TPU v7x, 32 devices: a whole 2x2x4 slice. The times are simulated.
32 devices in a mesh: groups: 2 (over x), gy: 16 (over z, y, core).
Axes of the slice: x: 2, y: 2, z: 4, core: 2. Of those that a mesh axis runs over, the one named last changes fastest.
Arguments:
- observed: float32 [2048, 16, 256], P(('groups', 'gy')), parts along dimension 0, may hold values from -6 to 6
- tf_table: float32 [16], replicated, may hold values from 0.2 to 2
- tilt_index: int32 [513, 129], replicated, may hold values from 0 to 15
- wedge: int32 [513, 129], replicated, may hold values 0 or 1
Outputs:
- restored: float32 [2048, 16, 256], P(('groups', 'gy')), parts along dimension 0
There are 2 independent parts, one for each index of `groups`. A program takes and returns all parts, laid end to end along the dimension named above; an argument that names none is the same for every part. Nothing has to cross between parts.
All inputs are finite; a program needn't handle non-finite values.
Results may differ from a plain program's by a relative error of at most 0.00011.
Values sent between devices are 32-bit elements; how exact they have to be, the bound alone decides.
A program may use at most 64 MiB of HBM per device.

v0:
```python
import functools
import math

import jax
import jax.numpy as jnp
import numpy as np
from jax import lax
from jax.experimental import pallas as pl
from jax.experimental.pallas import tpu as pltpu
from jax.sharding import PartitionSpec as P

OUTER = 2
PASSES = 2
GROUP = 8
LANES = 128
STEP = 2

step_dual = 0.14
step_primal = 0.14
huber_eps = 0.05
bound_dual = 0.5
relax = 1.0 / (1.0 + step_dual * huber_eps / bound_dual)
gain = step_dual * relax
MESH = pl.DeviceIdType.MESH
f32 = jnp.float32
bf16 = jnp.bfloat16


def split(value):
    high = value.astype(bf16)
    low = (value - high.astype(f32)).astype(bf16)
    return high, low


def dot3(a_high, a_low, b_high, b_low):
    dot = functools.partial(jnp.dot, preferred_element_type=f32)
    return dot(a_high, b_high) + (dot(a_high, b_low) + dot(a_low, b_high))


def kernel(
    n, rows, order,
    cells_ref, table_ref, tilt_ref, wedge_ref, cos_ref, sin_ref, cas_ref, case_ref, zh_ref, zl_ref,
    out_ref,
    gathered, total, data_term, prior_gain, x_high, x_low, m_high, m_low, back,
    target, halo, goal, field, lead, duals, current, code,
    send_sem, recv_sem, back_send, back_recv, halo_send, halo_recv,
):
    me = lax.axis_index("gy")
    chunks, slots = len(order), len(order[0])
    groups = chunks * slots
    seat = {g: (c, s) for c in range(chunks) for s, g in enumerate(order[c])}
    part = slots * GROUP
    ny, nz = out_ref.shape[0], out_ref.shape[2]
    nx = n * rows
    half = n // 2
    span_rows = n * part
    block = math.gcd(nx, 256)
    row_blocks = nx // block

    barrier = pltpu.get_barrier_semaphore()

    def greet(o, carry):
        pl.semaphore_signal(
            barrier, inc=1, device_id={"gy": lax.rem(me + o, n)}, device_id_type=MESH
        )
        return carry

    lax.fori_loop(1, n, greet, 0)

    def each_peer(action):
        def first(k, carry):
            action((1 - me // half) * half + lax.rem(me + k, half))
            return carry

        def second(k, carry):
            action((me // half) * half + lax.rem(me + k, half))
            return carry

        lax.fori_loop(0, half, first, 0)
        lax.fori_loop(1, half, second, 0)

    def every_other(action):
        def step(o, carry):
            action(lax.rem(me + o, n))
            return carry

        lax.fori_loop(1, n, step, 0)

    def forward_copy(c, peer, owner):
        return pltpu.make_async_remote_copy(
            src_ref=current.at[peer, c],
            dst_ref=gathered.at[c, owner],
            send_sem=send_sem.at[c, peer],
            recv_sem=recv_sem.at[c, owner],
            device_id={"gy": peer},
            device_id_type=MESH,
        )

    def back_copy(c, peer, owner):
        return pltpu.make_async_remote_copy(
            src_ref=back.at[c, peer],
            dst_ref=target.at[owner, c],
            send_sem=back_send.at[c, peer],
            recv_sem=back_recv.at[c, owner],
            device_id={"gy": peer},
            device_id_type=MESH,
        )

    def halo_copy(side):
        return pltpu.make_async_remote_copy(
            src_ref=target.at[:, 0, slots - 1 if side == 0 else 0],
            dst_ref=halo.at[side],
            send_sem=halo_send.at[side],
            recv_sem=halo_recv.at[side],
            device_id={"gy": lax.rem(me + (1 if side == 0 else n - 1), n)},
            device_id_type=MESH,
        )

    def send_forward(c):
        each_peer(lambda peer: forward_copy(c, peer, me).start())
        gathered[c, me] = current[me, c]

    def stage(y, carry):
        stride = ny * nz // LANES
        for z in range(nz // LANES):
            first = (y // GROUP * (nz // LANES) + z) * GROUP + y % GROUP
            lines = cells_ref[pl.ds(first, rows, stride=stride), :]
            for g, (c, s) in seat.items():
                current[y, c, s, :, z * LANES : (z + 1) * LANES] = lines[
                    g * GROUP : (g + 1) * GROUP, :
                ]
        return carry

    def make_tables():
        def body(m, carry):
            lines = jnp.concatenate(
                [
                    cos_ref[pl.ds(k, 1), :] * cas_ref[...] + sin_ref[pl.ds(k, 1), :] * case_ref[...]
                    for k in (2 * m, 2 * m + 1)
                ],
                axis=0,
            )
            at = pl.ds(pl.multiple_of(m * 2 * GROUP, 2 * GROUP), 2 * GROUP)
            x_high[at, :], x_low[at, :] = split(lines)
            return carry

        lax.fori_loop(0, nx // (2 * GROUP), body, 0)

    def make_filter():
        columns, lines = tilt_ref.shape
        code[...] = jnp.zeros_like(code)
        code[0:columns, 0:lines] = jnp.where(wedge_ref[...] == 0, 0, tilt_ref[...] + 1).astype(f32)
        width, depth = code.shape
        kz = lax.broadcasted_iota(jnp.int32, (nz, width), 0)
        pick_z = jnp.where(
            lax.broadcasted_iota(jnp.int32, (nz, width), 1) == jnp.minimum(kz, nz - kz), 1.0, 0.0
        ).astype(bf16)
        spread = jnp.dot(pick_z, code[...].astype(bf16), preferred_element_type=f32).astype(bf16)

        def body(b, carry):
            line = b * block + lax.broadcasted_iota(jnp.int32, (block, depth), 0)
            c = line // span_rows
            slot = line % part // GROUP
            group = slot if chunks == 1 else jnp.where(slot == 0, c, groups - 1 - c)
            kx = line % span_rows // part * rows + group * GROUP + line % GROUP
            column = lax.broadcasted_iota(jnp.int32, (block, depth), 1)
            pick_x = jnp.where(column == jnp.minimum(kx, nx - kx), 1.0, 0.0).astype(bf16)
            which = lax.dot_general(
                pick_x, spread, (((1,), (1,)), ((), ())), preferred_element_type=f32
            )
            response = jnp.zeros_like(which)
            for level in range(table_ref.shape[0]):
                response = jnp.where(which == level + 1.0, table_ref[level], response)
            prior = 1.0 / (response * response + 1.0)
            at = pl.ds(pl.multiple_of(b * block, block), block)
            prior_gain[at, :] = prior
            data_term[at, :] = response * prior
            return carry

        lax.fori_loop(0, row_blocks, body, 0)

    def filtered(outer):
        for c in range(chunks):
            every_other(lambda owner: forward_copy(c, owner, owner).wait_recv())
            high, low = split(gathered[c].reshape(span_rows, nz))
            high, low = split(dot3(high, low, zh_ref[...], zl_ref[...]))

            def body(b, carry):
                at = pl.ds(pl.multiple_of(b * block, block), block)
                span = pl.ds(c * span_rows, span_rows)
                spectrum = dot3(x_high[at, span], x_low[at, span], high, low)
                if c > 0:
                    spectrum = total[at, :] + spectrum
                if c < chunks - 1:
                    total[at, :] = spectrum
                    return carry
                if outer == 0:
                    spectrum = spectrum * gain
                    data_term[at, :] = data_term[at, :] * spectrum
                a_high, a_low = split(data_term[at, :] + prior_gain[at, :] * spectrum)
                m_high[at, :], m_low[at, :] = split(dot3(a_high, a_low, zh_ref[...], zl_ref[...]))
                return carry

            lax.fori_loop(0, row_blocks, body, 0)

    def send_back(c):
        step = math.gcd(span_rows, 256)

        def body(b, carry):
            line = pl.ds(pl.multiple_of(c * span_rows + b * step, step), step)
            lines = dot3(x_high[line, :], x_low[line, :], m_high[...], m_low[...])
            count = step // part
            at = pl.ds(pl.multiple_of(b * count, count), count)
            back[c, at] = lines.reshape(count, slots, GROUP, nz)
            return carry

        lax.fori_loop(0, span_rows // step, body, 0)
        each_peer(lambda peer: back_copy(c, peer, me).start())
        target[me, c] = back[c, me]

    def denoise(outer, index, spans):
        dual_x, dual_y, dual_z = duals[3 * index : 3 * index + 3]
        members = [(g, low <= g < high) for low, high in spans for g in range(low - 1, high + 1)]
        wide = len(members) * GROUP
        step = STEP * GROUP
        strips = [(r, min(r + step, wide)) for r in range(0, wide, step)]
        edge = members[0][0] < 0
        if edge:
            place = lax.broadcasted_iota(jnp.int32, (GROUP, nz), 0) * 0 + me
            inside = jnp.concatenate(
                [
                    jnp.where(place > 0, 1.0, 0.0)
                    if g < 0
                    else jnp.where(place < n - 1, 1.0, 0.0)
                    if g >= groups
                    else jnp.ones((GROUP, nz), f32)
                    for g, _ in members
                ],
                axis=0,
            )

        def sum_x(ref, y, start, stop):
            first, last = max(start - GROUP, 0), min(stop + GROUP, wide)
            value = ref[y, first:last, :]
            both = pltpu.roll(value, 1, 0) + pltpu.roll(value, last - first - 1, 0)
            return both[start - first : stop - first, :]

        def sum_z(value):
            pieces = [value[:, z : z + LANES] for z in range(0, nz, LANES)]
            nothing = jnp.zeros_like(pieces[0])
            lane = lax.broadcasted_iota(jnp.int32, pieces[0].shape, 1)
            ups = [nothing] + [pltpu.roll(piece, 1, 1) for piece in pieces]
            downs = [pltpu.roll(piece, LANES - 1, 1) for piece in pieces] + [nothing]
            return jnp.concatenate(
                [
                    jnp.where(lane == 0, ups[z], ups[z + 1])
                    + jnp.where(lane == LANES - 1, downs[z + 1], downs[z])
                    for z in range(len(pieces))
                ],
                axis=1,
            )

        def at_edge(start, stop):
            some = [g for g, _ in members[start // GROUP : stop // GROUP]]
            return min(some) < 0 or max(some) >= groups

        def collect(y, carry):
            pieces = []
            for g, _ in members:
                if g < 0:
                    pieces.append(halo[0, y])
                elif g >= groups:
                    pieces.append(halo[1, y])
                else:
                    pieces.append(target[y, seat[g][0], seat[g][1]])
            goal[y + 1, 0:wide, :] = jnp.concatenate(pieces, axis=0)
            return carry

        lax.fori_loop(0, ny, collect, 0)
        for sweep in range(PASSES):
            origin = goal if sweep == 0 else lead
            fresh = outer == 0 and sweep == 0

            def rise(y):
                for start, stop in strips:
                    here = origin[y, start:stop, :]
                    twice = here + here
                    raised = [
                        sum_x(origin, y, start, stop) - twice,
                        origin[y - 1, start:stop, :] + origin[y + 1, start:stop, :] - twice,
                        sum_z(here) - twice,
                    ]
                    if not fresh:
                        raised = [
                            dual[y, start:stop, :] + bend
                            for dual, bend in zip((dual_x, dual_y, dual_z), raised)
                        ]
                    norm = raised[0] * raised[0] + raised[1] * raised[1] + raised[2] * raised[2]
                    shrink = lax.rsqrt(
                        jnp.maximum(1.0 / relax**2, norm * (1.0 / (bound_dual * relax) ** 2))
                    )
                    if at_edge(start, stop):
                        shrink = shrink * inside[start:stop, :]
                    dual_x[y, start:stop, :] = raised[0] * shrink
                    dual_y[y, start:stop, :] = raised[1] * shrink
                    dual_z[y, start:stop, :] = raised[2] * shrink

            def fall(y):
                for start, stop in strips:
                    in_x, in_y, in_z = [
                        dual[y, start:stop, :] for dual in (dual_x, dual_y, dual_z)
                    ]
                    middle = in_x + in_y + in_z
                    adjoint = (
                        sum_x(dual_x, y, start, stop)
                        + (dual_y[y - 1, start:stop, :] + dual_y[y + 1, start:stop, :])
                        + sum_z(in_z)
                        - (middle + middle)
                    ) * (step_primal * step_dual / (1.0 + step_primal))
                    if sweep == 0:
                        old = goal[y, start:stop, :]
                        updated = old - adjoint
                    else:
                        old = field[y, start:stop, :]
                        updated = (
                            old * (1.0 / (1.0 + step_primal))
                            + goal[y, start:stop, :] * (step_primal / (1.0 + step_primal))
                            - adjoint
                        )
                    if sweep < PASSES - 1:
                        if at_edge(start, stop):
                            updated = updated * inside[start:stop, :]
                        lead[y, start:stop, :] = updated + updated - old
                        field[y, start:stop, :] = updated
                        continue
                    for i, (g, own) in enumerate(members):
                        if own and start <= i * GROUP < stop:
                            lines = updated[i * GROUP - start : (i + 1) * GROUP - start, :]
                            if outer < OUTER - 1:
                                current[y - 1, seat[g][0], seat[g][1]] = lines
                            else:
                                out_ref[y - 1, g * GROUP : (g + 1) * GROUP, :] = lines * (1.0 / gain)

            rise(1)

            def body(y, carry):
                rise(y)
                fall(y - 1)
                return carry

            lax.fori_loop(2, ny + 1, body, 0)
            fall(ny)

    lax.fori_loop(0, ny, stage, 0)
    pl.semaphore_wait(barrier, n - 1)
    for c in range(chunks):
        send_forward(c)

    @pl.when(me == 0)
    def _():
        halo[0] = jnp.zeros(halo.shape[1:], f32)

    @pl.when(me == n - 1)
    def _():
        halo[1] = jnp.zeros(halo.shape[1:], f32)

    for ref in [goal, lead] + list(duals[1::3]):
        ref[0] = jnp.zeros(ref.shape[1:], f32)
        ref[ny + 1] = jnp.zeros(ref.shape[1:], f32)
    make_tables()
    make_filter()
    quarter = groups // 4
    for outer in range(OUTER):
        filtered(outer)
        for c in range(chunks):
            every_other(lambda peer: forward_copy(c, peer, me).wait_send())
        for c in range(chunks):
            send_back(c)

        def arrive(some):
            for c in some:
                every_other(lambda owner: back_copy(c, owner, owner).wait_recv())

        arrive([0])

        @pl.when(me < n - 1)
        def _():
            halo_copy(0).start()

        @pl.when(me > 0)
        def _():
            halo_copy(1).start()

        early = list(range(1, quarter + 1)) if chunks > 1 else []
        arrive(early)

        @pl.when(me > 0)
        def _():
            halo_copy(0).wait_recv()

        @pl.when(me < n - 1)
        def _():
            halo_copy(1).wait_recv()

        done = 0
        if chunks > 1:
            done = quarter
            arrive(range(quarter + 1, chunks))
            denoise(outer, 0, [(0, groups)])
            done = 0
        else:
            denoise(outer, 0, [(0, groups)])

        @pl.when(me < n - 1)
        def _():
            halo_copy(0).wait_send()

        @pl.when(me > 0)
        def _():
            halo_copy(1).wait_send()

        for c in range(chunks):
            every_other(lambda peer: back_copy(c, peer, me).wait_send())
        if outer < OUTER - 1:
            for c in range(done, chunks):
                send_forward(c)


def constants(n, rows, order, nz):
    nx = n * rows
    place = np.array(
        [
            d * rows + g * GROUP + r
            for some in order
            for d in range(n)
            for g in some
            for r in range(GROUP)
        ]
    )
    turn = 2.0 * math.pi / nx
    coarse = (place[::GROUP, None] * place[None, :] % nx) * turn
    fine = (np.arange(GROUP)[:, None] * place[None, :] % nx) * turn
    norm = 1.0 / math.sqrt(nx)
    tables = (
        np.cos(coarse),
        np.sin(coarse),
        (np.cos(fine) + np.sin(fine)) * norm,
        (np.cos(fine) - np.sin(fine)) * norm,
    )
    k = np.arange(nz)
    angle = (k[:, None] * k[None, :] % nz) * (2.0 * math.pi / nz)
    cas_z = ((np.cos(angle) + np.sin(angle)) / math.sqrt(nz)).astype(np.float32)
    z_high = cas_z.astype(bf16)
    z_low = (cas_z - z_high.astype(np.float32)).astype(bf16)
    return [jnp.asarray(t, f32) for t in tables] + [jnp.asarray(z_high), jnp.asarray(z_low)]


def local(n, observed, tf_table, tilt_index, wedge):
    rows, ny, nz = observed.shape
    nx = n * rows
    groups = rows // GROUP
    if groups % 4 == 0:
        order = [(c, groups - 1 - c) for c in range(groups // 2)]
        sizes = [groups + 2]
    else:
        order = [tuple(range(groups))]
        sizes = [groups + 2]
    chunks, slots = len(order), len(order[0])
    lines, columns = tilt_index.shape
    depth, width = -(-lines // 128) * 128, -(-columns // 128) * 128
    tables = constants(n, rows, order, nz)
    tiles = observed.reshape(rows, ny // GROUP, GROUP, nz // LANES, LANES)
    tiles = tiles.transpose(0, 1, 3, 2, 4).reshape(-1, LANES)
    vmem = pl.BlockSpec(memory_space=pltpu.VMEM)
    smem = pl.BlockSpec(memory_space=pltpu.SMEM)
    tile_rows = [size * GROUP for size in sizes]
    scratch_tile = pltpu.VMEM((ny + 2, max(tile_rows), nz), f32)
    plane = pltpu.VMEM((nx, nz), f32)
    blocks = pltpu.VMEM((chunks, n, slots, GROUP, nz), f32)
    cells = pltpu.VMEM((ny, chunks, slots, GROUP, nz), f32)
    semaphores = pltpu.SemaphoreType.DMA((chunks, n))
    result = pl.pallas_call(
        functools.partial(kernel, n, rows, order),
        out_shape=jax.ShapeDtypeStruct((ny, rows, nz), f32),
        in_specs=[vmem, smem] + [vmem] * 8,
        out_specs=vmem,
        scratch_shapes=[
            blocks,
            plane,
            plane,
            plane,
            pltpu.VMEM((nx, nx), bf16),
            pltpu.VMEM((nx, nx), bf16),
            pltpu.VMEM((nx, nz), bf16),
            pltpu.VMEM((nx, nz), bf16),
            blocks,
            cells,
            pltpu.VMEM((2, ny, GROUP, nz), f32),
            scratch_tile,
            scratch_tile,
            scratch_tile,
            [pltpu.VMEM((ny + 2, size, nz), f32) for size in tile_rows for _ in range(3)],
            cells,
            pltpu.VMEM((width, depth), f32),
            semaphores,
            semaphores,
            semaphores,
            semaphores,
            pltpu.SemaphoreType.DMA((2,)),
            pltpu.SemaphoreType.DMA((2,)),
        ],
        compiler_params=pltpu.CompilerParams(
            collective_id=0, has_side_effects=True, vmem_limit_bytes=60 * 1024 * 1024
        ),
    )(tiles, tf_table, tilt_index.T, wedge.T, *tables)
    return jnp.swapaxes(result, 0, 1)


def solution(mesh):
    in_specs = (P(("groups", "gy"), None, None), P(), P(), P())
    out_specs = P(("groups", "gy"), None, None)
    body = functools.partial(local, mesh.shape["gy"])
    return jax.shard_map(body, mesh=mesh, in_specs=in_specs, out_specs=out_specs, check_vma=False)
```

profile of v0, /device:TPU:2, one launch (start us, length us, event | category | flops | bytes accessed | tf_op | source)
XLA Modules:
  0.0 135.1 jit_solution(18169351738180319720)
XLA Ops:
  0.0 132.2 %shard_map.100 = f32[16,64,256]{2,1,0:T(8,128)} custom-call(f32[2048,128]{1,0:T(8,128)} %bitcast.9, f32[16]{0:T(128)} %table_ref.1, s32[129,513]{1,0:T(8,128)} %bitcast.10, s32[129,513]{1,0:T(8,128)} %bitcast.11, f32[128,1024]{1,0:T(8,128)} %constant.12.clone.cos_ref, f32[128,1024]{1,0:T(8,128)} %constant.13.clone.sin_ref, ...), custom_call_target="tpu_custom_call" | custom-call | tf_op jit(solution)/shard_map/pallas_call | solution.py:482
  132.2 2.8 %copy.11 = f32[64,16,256]{2,1,0:T(8,128)} copy(f32[64,16,256]{2,0,1:T(8,128)} %bitcast.8) | data formatting | bytes 2097152 | tf_op jit(solution)/shard_map/transpose | solution.py:516
where the time goes:
time: 137 us; the launch traced here: 135 us
  Pallas kernels  132 us (96%)
  local copies, waits for them, and re-layouts  2.81 us (2%)
    pallas_call x1, Pallas kernels, local(): pl.pallas_call(functools.partial(kernel, n, rows, order), out_shape=jax.S...  132 us
    transpose x1, local copies, waits for them, and re-layouts, local(): return jnp.swapaxes(result, 0, 1)  2.81 us

commit v1 on v0

v1 whole, which is shorter than its diff:
```python
import functools
import math

import jax
import jax.numpy as jnp
import numpy as np
from jax import lax
from jax.experimental import pallas as pl
from jax.experimental.pallas import tpu as pltpu
from jax.sharding import PartitionSpec as P

OUTER = 2
PASSES = 2
GROUP = 8
LANES = 128
REACH = 6
PAD = 12

step_dual = 0.14
step_primal = 0.14
huber_eps = 0.05
bound_dual = 0.5
relax = 1.0 / (1.0 + step_dual * huber_eps / bound_dual)
gain = step_dual * relax
MESH = pl.DeviceIdType.MESH
f32 = jnp.float32
bf16 = jnp.bfloat16


def split(value):
    high = value.astype(bf16)
    low = (value - high.astype(f32)).astype(bf16)
    return high, low


def dot3(a_high, a_low, b_high, b_low):
    dot = functools.partial(jnp.dot, preferred_element_type=f32)
    return dot(a_high, b_high) + (dot(a_high, b_low) + dot(a_low, b_high))


def kernel(
    n, rows, order,
    cells_ref, table_ref, tilt_ref, wedge_ref, cos_ref, sin_ref, cas_ref, case_ref, zh_ref, zl_ref,
    out_ref,
    gathered, total, data_term, prior_gain, x_high, x_low, m_high, m_low, back,
    target, goal, field, lead, duals, current, code,
    send_sem, recv_sem, back_send, back_recv, halo_send, halo_recv,
):
    me = lax.axis_index("gy")
    chunks, slots = len(order), len(order[0])
    groups = chunks * slots
    part = slots * GROUP
    ny, nz = out_ref.shape[1], out_ref.shape[2]
    halves = nz // LANES
    deep = groups * GROUP * halves
    share = part * halves
    nx = n * rows
    half = n // 2
    span_rows = n * part
    block = math.gcd(nx, 256)
    row_blocks = nx // block

    barrier = pltpu.get_barrier_semaphore()

    def greet(o, carry):
        pl.semaphore_signal(
            barrier, inc=1, device_id={"gy": lax.rem(me + o, n)}, device_id_type=MESH
        )
        return carry

    lax.fori_loop(1, n, greet, 0)

    def each_peer(action):
        def first(k, carry):
            action((1 - me // half) * half + lax.rem(me + k, half))
            return carry

        def second(k, carry):
            action((me // half) * half + lax.rem(me + k, half))
            return carry

        lax.fori_loop(0, half, first, 0)
        lax.fori_loop(1, half, second, 0)

    def every_other(action):
        def step(o, carry):
            action(lax.rem(me + o, n))
            return carry

        lax.fori_loop(1, n, step, 0)

    def cells_of(y, c):
        return pl.ds(pl.multiple_of(y * deep + c * share, share), share)

    def block_of(device):
        return pl.ds(pl.multiple_of(device * share, share), share)

    def cell_row(x, h):
        place = lax.rem(x // GROUP + 1, groups)
        return (place * halves + h) * GROUP + lax.rem(x, GROUP)

    def forward_copy(c, peer, owner):
        return pltpu.make_async_remote_copy(
            src_ref=current.at[cells_of(peer, c)],
            dst_ref=gathered.at[c, block_of(owner)],
            send_sem=send_sem.at[c, peer],
            recv_sem=recv_sem.at[c, owner],
            device_id={"gy": peer},
            device_id_type=MESH,
        )

    def back_copy(c, peer, owner):
        return pltpu.make_async_remote_copy(
            src_ref=back.at[c, block_of(peer)],
            dst_ref=target.at[cells_of(owner, c)],
            send_sem=back_send.at[c, peer],
            recv_sem=back_recv.at[c, owner],
            device_id={"gy": peer},
            device_id_type=MESH,
        )

    def halo_copy(side):
        return pltpu.make_async_remote_copy(
            src_ref=goal.at[pl.ds(PAD + (rows - REACH if side == 0 else 0), REACH)],
            dst_ref=goal.at[pl.ds(PAD + (-REACH if side == 0 else rows), REACH)],
            send_sem=halo_send.at[side],
            recv_sem=halo_recv.at[side],
            device_id={"gy": lax.rem(me + (1 if side == 0 else n - 1), n)},
            device_id_type=MESH,
        )

    def send_forward(c):
        each_peer(lambda peer: forward_copy(c, peer, me).start())
        gathered[c, block_of(me)] = current[cells_of(me, c)]

    def stage(y, carry):
        stride = ny * halves
        for h in range(halves):
            first = (y // GROUP * halves + h) * GROUP + y % GROUP
            lines = cells_ref[pl.ds(first, rows, stride=stride), :]
            for g in range(groups):
                at = y * deep + ((g + 1) % groups * halves + h) * GROUP
                current[pl.ds(pl.multiple_of(at, GROUP), GROUP), :] = lines[
                    g * GROUP : (g + 1) * GROUP, :
                ]
        return carry

    def make_tables():
        def body(m, carry):
            lines = jnp.concatenate(
                [
                    cos_ref[pl.ds(k, 1), :] * cas_ref[...] + sin_ref[pl.ds(k, 1), :] * case_ref[...]
                    for k in (2 * m, 2 * m + 1)
                ],
                axis=0,
            )
            at = pl.ds(pl.multiple_of(m * 2 * GROUP, 2 * GROUP), 2 * GROUP)
            x_high[at, :], x_low[at, :] = split(lines)
            return carry

        lax.fori_loop(0, nx // (2 * GROUP), body, 0)

    def make_filter():
        columns, lines = tilt_ref.shape
        code[...] = jnp.zeros_like(code)
        code[0:columns, 0:lines] = jnp.where(wedge_ref[...] == 0, 0, tilt_ref[...] + 1).astype(f32)
        width, depth = code.shape
        kz = lax.broadcasted_iota(jnp.int32, (nz, width), 0)
        pick_z = jnp.where(
            lax.broadcasted_iota(jnp.int32, (nz, width), 1) == jnp.minimum(kz, nz - kz), 1.0, 0.0
        ).astype(bf16)
        spread = jnp.dot(pick_z, code[...].astype(bf16), preferred_element_type=f32).astype(bf16)

        def body(b, carry):
            line = b * block + lax.broadcasted_iota(jnp.int32, (block, depth), 0)
            c = line // span_rows
            slot = line % part // GROUP
            group = (c * slots + slot + groups - 1) % groups
            kx = line % span_rows // part * rows + group * GROUP + line % GROUP
            column = lax.broadcasted_iota(jnp.int32, (block, depth), 1)
            pick_x = jnp.where(column == jnp.minimum(kx, nx - kx), 1.0, 0.0).astype(bf16)
            which = lax.dot_general(
                pick_x, spread, (((1,), (1,)), ((), ())), preferred_element_type=f32
            )
            response = jnp.zeros_like(which)
            for level in range(table_ref.shape[0]):
                response = jnp.where(which == level + 1.0, table_ref[level], response)
            prior = 1.0 / (response * response + 1.0)
            at = pl.ds(pl.multiple_of(b * block, block), block)
            prior_gain[at, :] = prior
            data_term[at, :] = response * prior
            return carry

        lax.fori_loop(0, row_blocks, body, 0)

    def filtered(outer):
        turns = list(range(1, chunks)) + [0]
        for c in turns:
            every_other(lambda owner: forward_copy(c, owner, owner).wait_recv())
            pieces = gathered[c].reshape(n * slots, halves, GROUP, LANES)
            lines = [pieces[:, h].reshape(span_rows, LANES) for h in range(halves)]
            high, low = split(jnp.concatenate(lines, axis=1))
            high, low = split(dot3(high, low, zh_ref[...], zl_ref[...]))

            def body(b, carry):
                at = pl.ds(pl.multiple_of(b * block, block), block)
                span = pl.ds(c * span_rows, span_rows)
                spectrum = dot3(x_high[at, span], x_low[at, span], high, low)
                if c != turns[0]:
                    spectrum = total[at, :] + spectrum
                if c != turns[-1]:
                    total[at, :] = spectrum
                    return carry
                if outer == 0:
                    spectrum = spectrum * gain
                    data_term[at, :] = data_term[at, :] * spectrum
                a_high, a_low = split(data_term[at, :] + prior_gain[at, :] * spectrum)
                m_high[at, :], m_low[at, :] = split(dot3(a_high, a_low, zh_ref[...], zl_ref[...]))
                return carry

            lax.fori_loop(0, row_blocks, body, 0)

    def send_back(c):
        step = math.gcd(span_rows, 256)

        def body(b, carry):
            line = pl.ds(pl.multiple_of(c * span_rows + b * step, step), step)
            lines = dot3(x_high[line, :], x_low[line, :], m_high[...], m_low[...])
            pieces = [
                lines[:, h * LANES : (h + 1) * LANES].reshape(step // GROUP, 1, GROUP, LANES)
                for h in range(halves)
            ]
            count = step * halves
            at = pl.ds(pl.multiple_of(b * count, count), count)
            back[c, at] = jnp.concatenate(pieces, axis=1).reshape(count, LANES)
            return carry

        lax.fori_loop(0, span_rows // step, body, 0)
        each_peer(lambda peer: back_copy(c, peer, me).start())
        target[cells_of(me, c)] = back[c, block_of(me)]

    def sum_y(value):
        pieces = [value[y : y + GROUP, :] for y in range(0, ny, GROUP)]
        nothing = jnp.zeros_like(pieces[0])
        line = lax.broadcasted_iota(jnp.int32, pieces[0].shape, 0)
        ups = [nothing] + [pltpu.roll(piece, 1, 0) for piece in pieces]
        downs = [pltpu.roll(piece, GROUP - 1, 0) for piece in pieces] + [nothing]
        return jnp.concatenate(
            [
                jnp.where(line == 0, ups[y], ups[y + 1])
                + jnp.where(line == GROUP - 1, downs[y + 1], downs[y])
                for y in range(len(pieces))
            ],
            axis=0,
        )

    def sum_z(value):
        pieces = [value[:, z : z + LANES] for z in range(0, nz, LANES)]
        nothing = jnp.zeros_like(pieces[0])
        lane = lax.broadcasted_iota(jnp.int32, pieces[0].shape, 1)
        ups = [nothing] + [pltpu.roll(piece, 1, 1) for piece in pieces]
        downs = [pltpu.roll(piece, LANES - 1, 1) for piece in pieces] + [nothing]
        return jnp.concatenate(
            [
                jnp.where(lane == 0, ups[z], ups[z + 1])
                + jnp.where(lane == LANES - 1, downs[z + 1], downs[z])
                for z in range(len(pieces))
            ],
            axis=1,
        )

    def collect(c):
        def body(r, carry):
            for g in order[c]:
                for h in range(halves):
                    for y in range(0, ny, GROUP):
                        first = y * deep + ((g + 1) % groups * halves + h) * GROUP + r
                        goal[PAD + g * GROUP + r, y : y + GROUP, h * LANES : (h + 1) * LANES] = (
                            target[pl.ds(first, GROUP, stride=deep), :]
                        )
            return carry

        lax.fori_loop(0, GROUP, body, 0)

    def rise_load(origin, x, fresh):
        here, before, after = origin[x], origin[x - 1], origin[x + 1]
        olds = None if fresh else [dual[x] for dual in duals]
        return here, before, after, olds

    def rise(loaded, keep):
        here, before, after, olds = loaded
        twice = here + here
        raised = [before + after - twice, sum_y(here) - twice, sum_z(here) - twice]
        if olds is not None:
            raised = [old + bend for old, bend in zip(olds, raised)]
        norm = raised[0] * raised[0] + raised[1] * raised[1] + raised[2] * raised[2]
        shrink = lax.rsqrt(jnp.maximum(1.0 / relax**2, norm * (1.0 / (bound_dual * relax) ** 2)))
        if keep is not None:
            shrink = shrink * keep
        return [part_of * shrink for part_of in raised]

    def fall_load(x):
        dual_x, dual_y, dual_z = duals
        return (
            dual_x[x], dual_x[x - 1], dual_x[x + 1],
            dual_y[x], dual_z[x], goal[x],
        )

    def fall(loaded):
        in_x, before, after, in_y, in_z, _ = loaded
        middle = in_x + in_y + in_z
        return (before + after + sum_y(in_y) + sum_z(in_z) - (middle + middle)) * (
            step_primal * step_dual / (1.0 + step_primal)
        )

    def sweep_rows(outer, start, stop):
        def run(first, last):
            masked = first < REACH or last > rows
            ends = first >= REACH and last <= rows + REACH

            def keep(x):
                if not masked:
                    return None
                whole = me * rows + PAD + x
                return jnp.where(jnp.logical_and(whole >= 2 * PAD, whole < nx + 2 * PAD), 1.0, 0.0)

            def body(x, carry):
                low = rise_load(goal, x, outer == 0)
                mid = fall_load(x - 2)
                high = rise_load(lead, x - 4, False)
                if ends:
                    top = fall_load(x - 6)
                    old = field[x - 6]
                fresh = rise(low, keep(x))
                updated = mid[-1] - fall(mid)
                if masked:
                    updated = updated * keep(x - 2)
                again = rise(high, keep(x - 4))
                if ends:
                    final = (
                        old * (1.0 / (1.0 + step_primal))
                        + top[-1] * (step_primal / (1.0 + step_primal))
                        - fall(top)
                    )
                for dual, value in zip(duals, fresh):
                    dual[x] = value
                lead[x - 2] = updated + updated - mid[-1]
                field[x - 2] = updated
                for dual, value in zip(duals, again):
                    dual[x - 4] = value
                if ends and outer == OUTER - 1:
                    out_ref[x - PAD - 6] = final * (1.0 / gain)
                elif ends:
                    for h in range(halves):
                        at = cell_row(x - PAD - 6, h)
                        for y in range(0, ny, GROUP):
                            current[pl.ds(at + y * deep, GROUP, stride=deep), :] = final[
                                y : y + GROUP, h * LANES : (h + 1) * LANES
                            ]
                return carry

            lax.fori_loop(first + PAD, last + PAD, body, 0)

        marks = [start] + [x for x in (REACH, rows, rows + REACH) if start < x < stop] + [stop]
        for first, last in zip(marks[:-1], marks[1:]):
            run(first, last)

    def denoise(outer, arrive):
        stop = rows + REACH + (1 if outer < OUTER - 1 else 0)
        done = -5 if outer < OUTER - 1 else -3
        ready = {}
        if outer < OUTER - 1:
            for c in range(1, chunks):
                ready[(c * slots + slots - 1) * GROUP + REACH] = c
            ready[rows + REACH] = 0
        for c in range(min(1, chunks - 1), chunks):
            if c > 0:
                arrive(c)
                collect(c)
            if c == min(1, chunks - 1):
                halo_done()
            limit = stop if c == chunks - 1 else (c * slots + slots - 1) * GROUP - 1
            for x in sorted(ready):
                if done < x <= limit:
                    sweep_rows(outer, done, x)
                    send_forward(ready[x])
                    done = x
            if done < limit:
                sweep_rows(outer, done, limit)
                done = limit

    lax.fori_loop(0, ny, stage, 0)
    pl.semaphore_wait(barrier, n - 1)
    for c in list(range(1, chunks)) + [0]:
        send_forward(c)

    @pl.when(me == 0)
    def _():
        goal[PAD - REACH : PAD] = jnp.zeros((REACH, ny, nz), f32)

    @pl.when(me == n - 1)
    def _():
        goal[PAD + rows : PAD + rows + REACH] = jnp.zeros((REACH, ny, nz), f32)

    make_tables()
    make_filter()

    def halo_done():
        @pl.when(me > 0)
        def _():
            halo_copy(0).wait_recv()

        @pl.when(me < n - 1)
        def _():
            halo_copy(1).wait_recv()

    for outer in range(OUTER):
        filtered(outer)
        for c in range(chunks):
            every_other(lambda peer: forward_copy(c, peer, me).wait_send())
        for c in range(chunks):
            send_back(c)

        def arrive(c):
            every_other(lambda owner: back_copy(c, owner, owner).wait_recv())

        arrive(0)
        collect(0)

        @pl.when(me < n - 1)
        def _():
            halo_copy(0).start()

        @pl.when(me > 0)
        def _():
            halo_copy(1).start()

        denoise(outer, arrive)

        @pl.when(me < n - 1)
        def _():
            halo_copy(0).wait_send()

        @pl.when(me > 0)
        def _():
            halo_copy(1).wait_send()

        for c in range(chunks):
            every_other(lambda peer: back_copy(c, peer, me).wait_send())


def constants(n, rows, order, nz):
    nx = n * rows
    place = np.array(
        [
            d * rows + g * GROUP + r
            for some in order
            for d in range(n)
            for g in some
            for r in range(GROUP)
        ]
    )
    turn = 2.0 * math.pi / nx
    coarse = (place[::GROUP, None] * place[None, :] % nx) * turn
    fine = (np.arange(GROUP)[:, None] * place[None, :] % nx) * turn
    norm = 1.0 / math.sqrt(nx)
    tables = (
        np.cos(coarse),
        np.sin(coarse),
        (np.cos(fine) + np.sin(fine)) * norm,
        (np.cos(fine) - np.sin(fine)) * norm,
    )
    k = np.arange(nz)
    angle = (k[:, None] * k[None, :] % nz) * (2.0 * math.pi / nz)
    cas_z = ((np.cos(angle) + np.sin(angle)) / math.sqrt(nz)).astype(np.float32)
    z_high = cas_z.astype(bf16)
    z_low = (cas_z - z_high.astype(np.float32)).astype(bf16)
    return [jnp.asarray(t, f32) for t in tables] + [jnp.asarray(z_high), jnp.asarray(z_low)]


def local(n, observed, tf_table, tilt_index, wedge):
    rows, ny, nz = observed.shape
    nx = n * rows
    groups = rows // GROUP
    line = [groups - 1] + list(range(groups - 1))
    slots = 2 if groups % 2 == 0 else groups
    order = [tuple(line[c : c + slots]) for c in range(0, groups, slots)]
    chunks = len(order)
    lines, columns = tilt_index.shape
    depth, width = -(-lines // 128) * 128, -(-columns // 128) * 128
    tables = constants(n, rows, order, nz)
    tiles = observed.reshape(rows, ny // GROUP, GROUP, nz // LANES, LANES)
    tiles = tiles.transpose(0, 1, 3, 2, 4).reshape(-1, LANES)
    vmem = pl.BlockSpec(memory_space=pltpu.VMEM)
    smem = pl.BlockSpec(memory_space=pltpu.SMEM)
    grid_rows = pltpu.VMEM((rows + 2 * PAD, ny, nz), f32)
    plane = pltpu.VMEM((nx, nz), f32)
    blocks = pltpu.VMEM((chunks, n * slots * GROUP * nz // LANES, LANES), f32)
    cells = pltpu.VMEM((rows * ny * nz // LANES, LANES), f32)
    semaphores = pltpu.SemaphoreType.DMA((chunks, n))
    result = pl.pallas_call(
        functools.partial(kernel, n, rows, order),
        out_shape=jax.ShapeDtypeStruct((rows, ny, nz), f32),
        in_specs=[vmem, smem] + [vmem] * 8,
        out_specs=vmem,
        scratch_shapes=[
            blocks,
            plane,
            plane,
            plane,
            pltpu.VMEM((nx, nx), bf16),
            pltpu.VMEM((nx, nx), bf16),
            pltpu.VMEM((nx, nz), bf16),
            pltpu.VMEM((nx, nz), bf16),
            blocks,
            cells,
            grid_rows,
            grid_rows,
            grid_rows,
            [grid_rows] * 3,
            cells,
            pltpu.VMEM((width, depth), f32),
            semaphores,
            semaphores,
            semaphores,
            semaphores,
            pltpu.SemaphoreType.DMA((2,)),
            pltpu.SemaphoreType.DMA((2,)),
        ],
        compiler_params=pltpu.CompilerParams(
            collective_id=0, has_side_effects=True, vmem_limit_bytes=60 * 1024 * 1024
        ),
    )(tiles, tf_table, tilt_index.T, wedge.T, *tables)
    return result


def solution(mesh):
    in_specs = (P(("groups", "gy"), None, None), P(), P(), P())
    out_specs = P(("groups", "gy"), None, None)
    body = functools.partial(local, mesh.shape["gy"])
    return jax.shard_map(body, mesh=mesh, in_specs=in_specs, out_specs=out_specs, check_vma=False)
```

time: 137 us -> 127 us (0.927)
  the two profiles are of different devices: /device:TPU:2 before, /device:TPU:16 now
where the time goes in v1:
time: 127 us
  Pallas kernels  124 us (98%)
  local copies, waits for them, and re-layouts  2.26 us (2%)
    pallas_call x1, Pallas kernels, local(): pl.pallas_call(functools.partial(kernel, n, rows, order), out_shape=jax.S...  124 us

profile of v1, /device:TPU:16, one launch (start us, length us, event | category | flops | bytes accessed | tf_op | source)
XLA Modules:
  0.0 126.6 jit_solution(9767358254256952237)
XLA Ops:
  0.0 124.3 %shard_map.100 = f32[64,16,256]{2,1,0:T(8,128)} custom-call(f32[2048,128]{1,0:T(8,128)} %bitcast.7, f32[16]{0:T(128)} %table_ref.1, s32[129,513]{1,0:T(8,128)} %bitcast.8, s32[129,513]{1,0:T(8,128)} %bitcast.9, f32[128,1024]{1,0:T(8,128)} %constant.12.clone.cos_ref, f32[128,1024]{1,0:T(8,128)} %constant.13.clone.sin_ref, f32[8,1024]{1,0:T(8,128)} %constant.14.clone.cas_ref, ...), custom_call_target="tpu_custom_call" | custom-call | tf_op jit(solution)/shard_map/pallas_call | solution.py:501
  124.4 2.3 %copy.12 = f32[64,16,256]{2,1,0:T(8,128)} copy(f32[64,16,256]{2,1,0:T(8,128)} %shard_map.100) | data formatting | bytes 2097152

commit v2 on v1

--- a/solution.py
+++ b/solution.py
@@ -39,14 +39,38 @@
 
 
 def kernel(
-    n, rows, order,
+    n, rows, order, cross,
     cells_ref, table_ref, tilt_ref, wedge_ref, cos_ref, sin_ref, cas_ref, case_ref, zh_ref, zl_ref,
     out_ref,
     gathered, total, data_term, prior_gain, x_high, x_low, m_high, m_low, back,
-    target, goal, field, lead, duals, current, code,
+    target, goal, field, lead, duals, current, code, passing, result,
     send_sem, recv_sem, back_send, back_recv, halo_send, halo_recv,
+    pass_send, pass_recv, pass_on, home_send, home_recv, own_sem,
 ):
-    me = lax.axis_index("gy")
+    gx, gy = lax.axis_index("groups"), lax.axis_index("gy")
+    half = n // 2
+    high, low = gy // half, gy % half
+    if cross:
+        near = gx == high
+        who = gx * half + low
+        me = low % 2 * half + low // 2 * 2 + gx
+    else:
+        near = gx == gx
+        who = gy
+        me = gy
+    far = jnp.logical_not(near)
+
+    def owner_device(owner, first):
+        if not cross:
+            return {"gy": owner}
+        block = gx if first else high
+        return {"groups": owner // half, "gy": block * half + owner % half}
+
+    def slab_device(slab):
+        if not cross:
+            return {"gy": slab}
+        return {"groups": slab % 2, "gy": high * half + slab % half // 2 * 2 + slab // half}
+
     chunks, slots = len(order), len(order[0])
     groups = chunks * slots
     part = slots * GROUP
@@ -55,7 +79,6 @@
     deep = groups * GROUP * halves
     share = part * halves
     nx = n * rows
-    half = n // 2
     span_rows = n * part
     block = math.gcd(nx, 256)
     row_blocks = nx // block
@@ -63,31 +86,30 @@
     barrier = pltpu.get_barrier_semaphore()
 
     def greet(o, carry):
-        pl.semaphore_signal(
-            barrier, inc=1, device_id={"gy": lax.rem(me + o, n)}, device_id_type=MESH
-        )
+        if cross:
+            other = lax.rem(gx * n + gy + o, 2 * n)
+            device = {"groups": other // n, "gy": other % n}
+        else:
+            device = {"gy": lax.rem(gy + o, n)}
+        pl.semaphore_signal(barrier, inc=1, device_id=device, device_id_type=MESH)
         return carry
 
-    lax.fori_loop(1, n, greet, 0)
-
-    def each_peer(action):
-        def first(k, carry):
-            action((1 - me // half) * half + lax.rem(me + k, half))
+    greeted = 2 * n if cross else n
+    lax.fori_loop(1, greeted, greet, 0)
+
+    def every_other(mine, action):
+        def step(o, carry):
+            action(lax.rem(mine + o, n))
             return carry
 
-        def second(k, carry):
-            action((me // half) * half + lax.rem(me + k, half))
+        lax.fori_loop(1, n, step, 0)
+
+    def every_half(action):
+        def step(o, carry):
+            action(lax.rem(low + o, half))
             return carry
 
-        lax.fori_loop(0, half, first, 0)
-        lax.fori_loop(1, half, second, 0)
-
-    def every_other(action):
-        def step(o, carry):
-            action(lax.rem(me + o, n))
-            return carry
-
-        lax.fori_loop(1, n, step, 0)
+        lax.fori_loop(0, half, step, 0)
 
     def cells_of(y, c):
         return pl.ds(pl.multiple_of(y * deep + c * share, share), share)
@@ -99,23 +121,43 @@
         place = lax.rem(x // GROUP + 1, groups)
         return (place * halves + h) * GROUP + lax.rem(x, GROUP)
 
-    def forward_copy(c, peer, owner):
+    def forward_copy(c, owner, slab, first):
         return pltpu.make_async_remote_copy(
-            src_ref=current.at[cells_of(peer, c)],
-            dst_ref=gathered.at[c, block_of(owner)],
-            send_sem=send_sem.at[c, peer],
-            recv_sem=recv_sem.at[c, owner],
-            device_id={"gy": peer},
+            src_ref=current.at[cells_of(owner, c)],
+            dst_ref=gathered.at[c, block_of(slab)],
+            send_sem=send_sem.at[c, owner],
+            recv_sem=recv_sem.at[c, slab],
+            device_id=owner_device(owner, first),
             device_id_type=MESH,
         )
 
-    def back_copy(c, peer, owner):
+    def pass_copy(c, k):
         return pltpu.make_async_remote_copy(
-            src_ref=back.at[c, block_of(peer)],
+            src_ref=current.at[cells_of((1 - gx) * half + k, c)],
+            dst_ref=passing.at[cells_of(k, c)],
+            send_sem=pass_send.at[c, k],
+            recv_sem=pass_recv.at[c, k],
+            device_id={"groups": 1 - gx, "gy": gy},
+            device_id_type=MESH,
+        )
+
+    def pass_on_copy(c, k):
+        return pltpu.make_async_remote_copy(
+            src_ref=passing.at[cells_of(k, c)],
+            dst_ref=gathered.at[c, block_of(gy)],
+            send_sem=pass_on.at[c, k],
+            recv_sem=recv_sem.at[c, gy],
+            device_id={"groups": gx, "gy": (1 - gx) * half + k},
+            device_id_type=MESH,
+        )
+
+    def back_copy(c, slab, owner):
+        return pltpu.make_async_remote_copy(
+            src_ref=back.at[c, block_of(slab)],
             dst_ref=target.at[cells_of(owner, c)],
-            send_sem=back_send.at[c, peer],
+            send_sem=back_send.at[c, slab],
             recv_sem=back_recv.at[c, owner],
-            device_id={"gy": peer},
+            device_id=slab_device(slab),
             device_id_type=MESH,
         )
 
@@ -125,13 +167,103 @@
             dst_ref=goal.at[pl.ds(PAD + (-REACH if side == 0 else rows), REACH)],
             send_sem=halo_send.at[side],
             recv_sem=halo_recv.at[side],
-            device_id={"gy": lax.rem(me + (1 if side == 0 else n - 1), n)},
+            device_id=slab_device(lax.rem(me + (1 if side == 0 else n - 1), n)),
             device_id_type=MESH,
         )
 
+    def home_copy(i, first, last):
+        span = pl.ds(first, last - first)
+        return pltpu.make_async_remote_copy(
+            src_ref=result.at[span],
+            dst_ref=out_ref.at[span],
+            send_sem=home_send.at[i],
+            recv_sem=home_recv.at[i],
+            device_id={"groups": high, "gy": me},
+            device_id_type=MESH,
+        )
+
+    def own_copy(i, first, last):
+        span = pl.ds(first, last - first)
+        return pltpu.make_async_copy(result.at[span], out_ref.at[span], own_sem.at[i])
+
+    if cross:
+        home = jnp.logical_and(gx == high, gy == me)
+        away = jnp.logical_not(home)
+    else:
+        home, away = near, far
+
+    def deliver(i, first, last):
+        if cross:
+
+            @pl.when(away)
+            def _():
+                home_copy(i, first, last).start()
+
+        @pl.when(home)
+        def _():
+            own_copy(i, first, last).start()
+
+    def delivered(i, first, last):
+        if cross:
+
+            @pl.when(away)
+            def _():
+                home_copy(i, first, last).wait_send()
+                home_copy(i, first, last).wait_recv()
+
+        @pl.when(home)
+        def _():
+            own_copy(i, first, last).wait()
+
+    def send_first(c):
+        if cross:
+
+            @pl.when(far)
+            def _():
+                every_half(lambda k: pass_copy(c, k).start())
+                every_half(lambda k: forward_copy(c, gx * half + k, gy, True).start())
+
+        @pl.when(near)
+        def _():
+            every_other(who, lambda owner: forward_copy(c, owner, gy, True).start())
+            gathered[c, block_of(gy)] = current[cells_of(who, c)]
+
+    def pass_along(c):
+        if cross:
+
+            @pl.when(near)
+            def _():
+                def step(k):
+                    pass_copy(c, k).wait_recv()
+                    pass_on_copy(c, k).start()
+
+                every_half(step)
+
+    def first_arrived(c):
+        every_other(gy, lambda slab: forward_copy(c, who, slab, True).wait_recv())
+        if cross:
+
+            @pl.when(far)
+            def _():
+                forward_copy(c, who, gy, True).wait_recv()
+
+    def first_sent(c):
+        if cross:
+
+            @pl.when(far)
+            def _():
+                every_half(lambda k: pass_copy(c, k).wait_send())
+                every_half(lambda k: forward_copy(c, gx * half + k, gy, True).wait_send())
+
+        @pl.when(near)
+        def _():
+            every_other(who, lambda owner: forward_copy(c, owner, gy, True).wait_send())
+            if cross:
+                every_half(lambda k: pass_on_copy(c, k).wait_send())
+
     def send_forward(c):
-        each_peer(lambda peer: forward_copy(c, peer, me).start())
-        gathered[c, block_of(me)] = current[cells_of(me, c)]
+        every_other(who, lambda owner: forward_copy(c, owner, me, False).start())
+        gathered[c, block_of(me)] = current[cells_of(who, c)]
 
     def stage(y, carry):
         stride = ny * halves
@@ -194,9 +326,11 @@
         lax.fori_loop(0, row_blocks, body, 0)
 
     def filtered(outer):
-        turns = list(range(1, chunks)) + [0]
         for c in turns:
-            every_other(lambda owner: forward_copy(c, owner, owner).wait_recv())
+            if outer == 0:
+                first_arrived(c)
+            else:
+                every_other(me, lambda slab: forward_copy(c, who, slab, False).wait_recv())
             pieces = gathered[c].reshape(n * slots, halves, GROUP, LANES)
             lines = [pieces[:, h].reshape(span_rows, LANES) for h in range(halves)]
             high, low = split(jnp.concatenate(lines, axis=1))
@@ -236,8 +370,8 @@
             return carry
 
         lax.fori_loop(0, span_rows // step, body, 0)
-        each_peer(lambda peer: back_copy(c, peer, me).start())
-        target[cells_of(me, c)] = back[c, block_of(me)]
+        every_other(me, lambda slab: back_copy(c, slab, who).start())
+        target[cells_of(who, c)] = back[c, block_of(me)]
 
     def sum_y(value):
         pieces = [value[y : y + GROUP, :] for y in range(0, ny, GROUP)]
@@ -349,7 +483,7 @@
                 for dual, value in zip(duals, again):
                     dual[x - 4] = value
                 if ends and outer == OUTER - 1:
-                    out_ref[x - PAD - 6] = final * (1.0 / gain)
+                    result[x - PAD - 6] = final * (1.0 / gain)
                 elif ends:
                     for h in range(halves):
                         at = cell_row(x - PAD - 6, h)
@@ -365,6 +499,8 @@
         for first, last in zip(marks[:-1], marks[1:]):
             run(first, last)
 
+    homes = [(x, x + GROUP) for x in range(0, rows, GROUP)]
+
     def denoise(outer, arrive):
         stop = rows + REACH + (1 if outer < OUTER - 1 else 0)
         done = -5 if outer < OUTER - 1 else -3
@@ -373,6 +509,8 @@
             for c in range(1, chunks):
                 ready[(c * slots + slots - 1) * GROUP + REACH] = c
             ready[rows + REACH] = 0
+        else:
+            ready = {last + REACH: i for i, (_, last) in enumerate(homes)}
         for c in range(min(1, chunks - 1), chunks):
             if c > 0:
                 arrive(c)
@@ -383,16 +521,20 @@
             for x in sorted(ready):
                 if done < x <= limit:
                     sweep_rows(outer, done, x)
-                    send_forward(ready[x])
+                    if outer < OUTER - 1:
+                        send_forward(ready[x])
+                    else:
+                        deliver(ready[x], *homes[ready[x]])
                     done = x
             if done < limit:
                 sweep_rows(outer, done, limit)
                 done = limit
 
+    turns = list(range(1, chunks)) + [0]
     lax.fori_loop(0, ny, stage, 0)
-    pl.semaphore_wait(barrier, n - 1)
-    for c in list(range(1, chunks)) + [0]:
-        send_forward(c)
+    pl.semaphore_wait(barrier, greeted - 1)
+    for c in turns:
+        send_first(c)
 
     @pl.when(me == 0)
     def _():
@@ -403,7 +545,11 @@
         goal[PAD + rows : PAD + rows + REACH] = jnp.zeros((REACH, ny, nz), f32)
 
     make_tables()
+    for c in turns[: chunks // 2]:
+        pass_along(c)
     make_filter()
+    for c in turns[chunks // 2 :]:
+        pass_along(c)
 
     def halo_done():
         @pl.when(me > 0)
@@ -417,12 +563,15 @@
     for outer in range(OUTER):
         filtered(outer)
         for c in range(chunks):
-            every_other(lambda peer: forward_copy(c, peer, me).wait_send())
+            if outer == 0:
+                first_sent(c)
+            else:
+                every_other(who, lambda owner: forward_copy(c, owner, me, False).wait_send())
         for c in range(chunks):
             send_back(c)
 
         def arrive(c):
-            every_other(lambda owner: back_copy(c, owner, owner).wait_recv())
+            every_other(who, lambda owner: back_copy(c, me, owner).wait_recv())
 
         arrive(0)
         collect(0)
@@ -446,7 +595,9 @@
             halo_copy(1).wait_send()
 
         for c in range(chunks):
-            every_other(lambda peer: back_copy(c, peer, me).wait_send())
+            every_other(me, lambda slab: back_copy(c, slab, who).wait_send())
+    for i, (first, last) in enumerate(homes):
+        delivered(i, first, last)
 
 
 def constants(n, rows, order, nz):
@@ -478,7 +629,7 @@
     return [jnp.asarray(t, f32) for t in tables] + [jnp.asarray(z_high), jnp.asarray(z_low)]
 
 
-def local(n, observed, tf_table, tilt_index, wedge):
+def local(n, cross, observed, tf_table, tilt_index, wedge):
     rows, ny, nz = observed.shape
     nx = n * rows
     groups = rows // GROUP
@@ -499,10 +650,10 @@
     cells = pltpu.VMEM((rows * ny * nz // LANES, LANES), f32)
     semaphores = pltpu.SemaphoreType.DMA((chunks, n))
     result = pl.pallas_call(
-        functools.partial(kernel, n, rows, order),
+        functools.partial(kernel, n, rows, order, cross),
         out_shape=jax.ShapeDtypeStruct((rows, ny, nz), f32),
         in_specs=[vmem, smem] + [vmem] * 8,
-        out_specs=vmem,
+        out_specs=pl.BlockSpec(memory_space=pl.ANY),
         scratch_shapes=[
             blocks,
             plane,
@@ -520,12 +671,20 @@
             [grid_rows] * 3,
             cells,
             pltpu.VMEM((width, depth), f32),
+            pltpu.VMEM((rows * ny * nz // LANES // 2, LANES), f32),
+            pltpu.VMEM((rows, ny, nz), f32),
             semaphores,
             semaphores,
             semaphores,
             semaphores,
             pltpu.SemaphoreType.DMA((2,)),
             pltpu.SemaphoreType.DMA((2,)),
+            pltpu.SemaphoreType.DMA((chunks, n // 2)),
+            pltpu.SemaphoreType.DMA((chunks, n // 2)),
+            pltpu.SemaphoreType.DMA((chunks, n // 2)),
+            pltpu.SemaphoreType.DMA((groups,)),
+            pltpu.SemaphoreType.DMA((groups,)),
+            pltpu.SemaphoreType.DMA((groups,)),
         ],
         compiler_params=pltpu.CompilerParams(
             collective_id=0, has_side_effects=True, vmem_limit_bytes=60 * 1024 * 1024
@@ -537,5 +696,7 @@
 def solution(mesh):
     in_specs = (P(("groups", "gy"), None, None), P(), P(), P())
     out_specs = P(("groups", "gy"), None, None)
-    body = functools.partial(local, mesh.shape["gy"])
+    n = mesh.shape["gy"]
+    cross = mesh.shape["groups"] == 2 and n % 4 == 0
+    body = functools.partial(local, n, cross)
     return jax.shard_map(body, mesh=mesh, in_specs=in_specs, out_specs=out_specs, check_vma=False)

time: 127 us -> 132 us (1.039)
  the two profiles are of different devices: /device:TPU:16 before, /device:TPU:2 now
where the time goes in v2:
time: 132 us; the launch traced here: 130 us
  Pallas kernels  128 us (97%)
  local copies, waits for them, and re-layouts  2.26 us (2%)
    pallas_call x1, Pallas kernels, local(): pl.pallas_call(functools.partial(kernel, n, rows, order, cross), out_shap...  128 us

profile of v2, /device:TPU:2, one launch (start us, length us, event | category | flops | bytes accessed | tf_op | source)
XLA Modules:
  0.0 130.5 jit_solution(1381053791360038137)
XLA Ops:
  0.0 128.2 %shard_map.100 = f32[64,16,256]{2,1,0:T(8,128)} custom-call(f32[2048,128]{1,0:T(8,128)} %bitcast.7, f32[16]{0:T(128)} %table_ref.1, s32[129,513]{1,0:T(8,128)} %bitcast.8, s32[129,513]{1,0:T(8,128)} %bitcast.9, f32[128,1024]{1,0:T(8,128)} %constant.12.clone.cos_ref, f32[128,1024]{1,0:T(8,128)} %constant.13.clone.sin_ref, f32[8,1024]{1,0:T(8,128)} %constant.14.clone.cas_ref, ...), custom_call_target="tpu_custom_call" | custom-call | tf_op jit(solution)/shard_map/pallas_call | solution.py:652
  128.2 2.3 %copy.12 = f32[64,16,256]{2,1,0:T(8,128)} copy(f32[64,16,256]{2,1,0:T(8,128)} %shard_map.100) | data formatting | bytes 2097152

commit v3 on v2

--- a/solution.py
+++ b/solution.py
@@ -39,12 +39,12 @@
 
 
 def kernel(
-    n, rows, order, cross,
+    n, rows, slots, cross,
     cells_ref, table_ref, tilt_ref, wedge_ref, cos_ref, sin_ref, cas_ref, case_ref, zh_ref, zl_ref,
     out_ref,
     gathered, total, data_term, prior_gain, x_high, x_low, m_high, m_low, back,
     target, goal, field, lead, duals, current, code, passing, result,
-    send_sem, recv_sem, back_send, back_recv, halo_send, halo_recv,
+    send_sem, recv_sem, back_send, back_recv,
     pass_send, pass_recv, pass_on, home_send, home_recv, own_sem,
 ):
     gx, gy = lax.axis_index("groups"), lax.axis_index("gy")
@@ -71,13 +71,22 @@
             return {"gy": slab}
         return {"groups": slab % 2, "gy": high * half + slab % half // 2 * 2 + slab // half}
 
-    chunks, slots = len(order), len(order[0])
-    groups = chunks * slots
+    groups = rows // GROUP
+    chunks = groups // slots
+    extents = (groups + 2) // slots
     part = slots * GROUP
     ny, nz = out_ref.shape[1], out_ref.shape[2]
     halves = nz // LANES
-    deep = groups * GROUP * halves
-    share = part * halves
+    tall = GROUP * halves
+    deep = groups * tall
+    wide = (groups + 2) * tall
+    share = slots * tall
+    batches = [
+        (m, max(m * slots - 1, 0), min((m + 1) * slots - 1, groups))
+        for m in range(1 // slots, groups // slots + 1)
+    ]
+    first_turn = [batch for batch in batches if batch[0] % chunks > 0]
+    first_turn += [batch for batch in batches if batch[0] % chunks == 0]
     nx = n * rows
     span_rows = n * part
     block = math.gcd(nx, 256)
@@ -111,80 +120,81 @@
 
         lax.fori_loop(0, half, step, 0)
 
-    def cells_of(y, c):
-        return pl.ds(pl.multiple_of(y * deep + c * share, share), share)
-
-    def block_of(device):
-        return pl.ds(pl.multiple_of(device * share, share), share)
+    def cells_of(y, batch, depth):
+        _, low_group, high_group = batch
+        return pl.ds(pl.multiple_of(y * depth + low_group * tall, tall), (high_group - low_group) * tall)
+
+    def seat_of(slab, batch):
+        m, low_group, high_group = batch
+        line = lax.rem(slab + m // chunks, n) * slots + (low_group + 1) % slots
+        return pl.ds(pl.multiple_of(line * tall, tall), (high_group - low_group) * tall)
+
+    def block_of(j, slab):
+        return pl.ds(pl.multiple_of(lax.rem(slab + j // chunks, n) * share, share), share)
+
+    def extent_of(y, j):
+        return pl.ds(pl.multiple_of(y * wide + j * share, tall), share)
 
     def cell_row(x, h):
-        place = lax.rem(x // GROUP + 1, groups)
-        return (place * halves + h) * GROUP + lax.rem(x, GROUP)
-
-    def forward_copy(c, owner, slab, first):
+        return (x // GROUP * halves + h) * GROUP + lax.rem(x, GROUP)
+
+    def forward_copy(batch, owner, slab, first):
+        m = batch[0]
         return pltpu.make_async_remote_copy(
-            src_ref=current.at[cells_of(owner, c)],
-            dst_ref=gathered.at[c, block_of(slab)],
-            send_sem=send_sem.at[c, owner],
-            recv_sem=recv_sem.at[c, slab],
+            src_ref=current.at[cells_of(owner, batch, deep)],
+            dst_ref=gathered.at[m % chunks, seat_of(slab, batch)],
+            send_sem=send_sem.at[m],
+            recv_sem=recv_sem.at[m],
             device_id=owner_device(owner, first),
             device_id_type=MESH,
         )
 
-    def pass_copy(c, k):
+    def pass_copy(batch, k):
+        m = batch[0]
         return pltpu.make_async_remote_copy(
-            src_ref=current.at[cells_of((1 - gx) * half + k, c)],
-            dst_ref=passing.at[cells_of(k, c)],
-            send_sem=pass_send.at[c, k],
-            recv_sem=pass_recv.at[c, k],
+            src_ref=current.at[cells_of((1 - gx) * half + k, batch, deep)],
+            dst_ref=passing.at[cells_of(k, batch, deep)],
+            send_sem=pass_send.at[m],
+            recv_sem=pass_recv.at[m],
             device_id={"groups": 1 - gx, "gy": gy},
             device_id_type=MESH,
         )
 
-    def pass_on_copy(c, k):
+    def pass_on_copy(batch, k):
+        m = batch[0]
         return pltpu.make_async_remote_copy(
-            src_ref=passing.at[cells_of(k, c)],
-            dst_ref=gathered.at[c, block_of(gy)],
-            send_sem=pass_on.at[c, k],
-            recv_sem=recv_sem.at[c, gy],
+            src_ref=passing.at[cells_of(k, batch, deep)],
+            dst_ref=gathered.at[m % chunks, seat_of(gy, batch)],
+            send_sem=pass_on.at[m],
+            recv_sem=recv_sem.at[m],
             device_id={"groups": gx, "gy": (1 - gx) * half + k},
             device_id_type=MESH,
         )
 
-    def back_copy(c, slab, owner):
+    def back_copy(j, slab):
         return pltpu.make_async_remote_copy(
-            src_ref=back.at[c, block_of(slab)],
-            dst_ref=target.at[cells_of(owner, c)],
-            send_sem=back_send.at[c, slab],
-            recv_sem=back_recv.at[c, owner],
+            src_ref=back.at[j % chunks, block_of(j, slab)],
+            dst_ref=target.at[extent_of(who, j)],
+            send_sem=back_send.at[j],
+            recv_sem=back_recv.at[j],
             device_id=slab_device(slab),
             device_id_type=MESH,
         )
 
-    def halo_copy(side):
-        return pltpu.make_async_remote_copy(
-            src_ref=goal.at[pl.ds(PAD + (rows - REACH if side == 0 else 0), REACH)],
-            dst_ref=goal.at[pl.ds(PAD + (-REACH if side == 0 else rows), REACH)],
-            send_sem=halo_send.at[side],
-            recv_sem=halo_recv.at[side],
-            device_id=slab_device(lax.rem(me + (1 if side == 0 else n - 1), n)),
-            device_id_type=MESH,
-        )
-
-    def home_copy(i, first, last):
+    def home_copy(first, last):
         span = pl.ds(first, last - first)
         return pltpu.make_async_remote_copy(
             src_ref=result.at[span],
             dst_ref=out_ref.at[span],
-            send_sem=home_send.at[i],
-            recv_sem=home_recv.at[i],
+            send_sem=home_send,
+            recv_sem=home_recv,
             device_id={"groups": high, "gy": me},
             device_id_type=MESH,
         )
 
-    def own_copy(i, first, last):
+    def own_copy(first, last):
         span = pl.ds(first, last - first)
-        return pltpu.make_async_copy(result.at[span], out_ref.at[span], own_sem.at[i])
+        return pltpu.make_async_copy(result.at[span], out_ref.at[span], own_sem)
 
     if cross:
         home = jnp.logical_and(gx == high, gy == me)
@@ -192,78 +202,116 @@
     else:
         home, away = near, far
 
-    def deliver(i, first, last):
+    def deliver(first, last):
         if cross:
 
             @pl.when(away)
             def _():
-                home_copy(i, first, last).start()
+                home_copy(first, last).start()
 
         @pl.when(home)
         def _():
-            own_copy(i, first, last).start()
-
-    def delivered(i, first, last):
+            own_copy(first, last).start()
+
+    def delivered():
         if cross:
 
             @pl.when(away)
             def _():
-                home_copy(i, first, last).wait_send()
-                home_copy(i, first, last).wait_recv()
+                home_copy(0, rows).wait_send()
+                home_copy(0, rows).wait_recv()
 
         @pl.when(home)
         def _():
-            own_copy(i, first, last).wait()
-
-    def send_first(c):
+            own_copy(0, rows).wait()
+
+    def bulk(ref, lines, send, recv):
+        span = ref.at[pl.ds(0, lines)]
+        return pltpu.make_async_remote_copy(
+            src_ref=span,
+            dst_ref=span,
+            send_sem=send,
+            recv_sem=recv,
+            device_id=owner_device(who, False),
+            device_id_type=MESH,
+        )
+
+    def lines_of(batch):
+        return (batch[2] - batch[1]) * tall
+
+    def forward_bulk(batch, count):
+        m = batch[0]
+        return bulk(current, count * lines_of(batch), send_sem.at[m], recv_sem.at[m])
+
+    def pass_bulk(batch):
+        m = batch[0]
+        return bulk(passing, half * lines_of(batch), pass_send.at[m], pass_recv.at[m])
+
+    def pass_on_bulk(batch):
+        m = batch[0]
+        return bulk(passing, half * lines_of(batch), pass_on.at[m], pass_recv.at[m])
+
+    def back_bulk(j):
+        return bulk(target, (n - 1) * share, back_send.at[j], back_recv.at[j])
+
+    def keep_own(batch, slab):
+        gathered[batch[0] % chunks, seat_of(slab, batch)] = current[cells_of(who, batch, deep)]
+
+    def send_direct(batch):
         if cross:
 
             @pl.when(far)
             def _():
-                every_half(lambda k: pass_copy(c, k).start())
-                every_half(lambda k: forward_copy(c, gx * half + k, gy, True).start())
+                every_half(lambda k: forward_copy(batch, gx * half + k, gy, True).start())
 
         @pl.when(near)
         def _():
-            every_other(who, lambda owner: forward_copy(c, owner, gy, True).start())
-            gathered[c, block_of(gy)] = current[cells_of(who, c)]
-
-    def pass_along(c):
+            every_other(who, lambda owner: forward_copy(batch, owner, gy, True).start())
+            keep_own(batch, gy)
+
+    def send_aside(batch):
+        if cross:
+
+            @pl.when(far)
+            def _():
+                every_half(lambda k: pass_copy(batch, k).start())
+
+    def pass_along(batch):
         if cross:
 
             @pl.when(near)
             def _():
-                def step(k):
-                    pass_copy(c, k).wait_recv()
-                    pass_on_copy(c, k).start()
-
-                every_half(step)
-
-    def first_arrived(c):
-        every_other(gy, lambda slab: forward_copy(c, who, slab, True).wait_recv())
+                pass_bulk(batch).wait_recv()
+                every_half(lambda k: pass_on_copy(batch, k).start())
+
+    def first_arrived(batch):
+        @pl.when(near)
+        def _():
+            forward_bulk(batch, n - 1).wait_recv()
+
         if cross:
 
             @pl.when(far)
             def _():
-                forward_copy(c, who, gy, True).wait_recv()
-
-    def first_sent(c):
+                forward_bulk(batch, n).wait_recv()
+
+    def first_sent(batch):
+        @pl.when(near)
+        def _():
+            forward_bulk(batch, n - 1).wait_send()
+            if cross:
+                pass_on_bulk(batch).wait_send()
+
         if cross:
 
             @pl.when(far)
             def _():
-                every_half(lambda k: pass_copy(c, k).wait_send())
-                every_half(lambda k: forward_copy(c, gx * half + k, gy, True).wait_send())
-
-        @pl.when(near)
-        def _():
-            every_other(who, lambda owner: forward_copy(c, owner, gy, True).wait_send())
-            if cross:
-                every_half(lambda k: pass_on_copy(c, k).wait_send())
-
-    def send_forward(c):
-        every_other(who, lambda owner: forward_copy(c, owner, me, False).start())
-        gathered[c, block_of(me)] = current[cells_of(who, c)]
+                forward_bulk(batch, half).wait_send()
+                pass_bulk(batch).wait_send()
+
+    def send_forward(batch):
+        every_other(who, lambda owner: forward_copy(batch, owner, me, False).start())
+        keep_own(batch, me)
 
     def stage(y, carry):
         stride = ny * halves
@@ -271,7 +319,7 @@
             first = (y // GROUP * halves + h) * GROUP + y % GROUP
             lines = cells_ref[pl.ds(first, rows, stride=stride), :]
             for g in range(groups):
-                at = y * deep + ((g + 1) % groups * halves + h) * GROUP
+                at = y * deep + g * tall + h * GROUP
                 current[pl.ds(pl.multiple_of(at, GROUP), GROUP), :] = lines[
                     g * GROUP : (g + 1) * GROUP, :
                 ]
@@ -307,8 +355,8 @@
             line = b * block + lax.broadcasted_iota(jnp.int32, (block, depth), 0)
             c = line // span_rows
             slot = line % part // GROUP
-            group = (c * slots + slot + groups - 1) % groups
-            kx = line % span_rows // part * rows + group * GROUP + line % GROUP
+            place = line % span_rows // part * groups + c * slots + slot - 1
+            kx = (place * GROUP + line % GROUP + nx) % nx
             column = lax.broadcasted_iota(jnp.int32, (block, depth), 1)
             pick_x = jnp.where(column == jnp.minimum(kx, nx - kx), 1.0, 0.0).astype(bf16)
             which = lax.dot_general(
@@ -327,10 +375,11 @@
 
     def filtered(outer):
         for c in turns:
-            if outer == 0:
-                first_arrived(c)
-            else:
-                every_other(me, lambda slab: forward_copy(c, who, slab, False).wait_recv())
+            for batch in batches:
+                if batch[0] % chunks == c and outer == 0:
+                    first_arrived(batch)
+                elif batch[0] % chunks == c:
+                    forward_bulk(batch, n - 1).wait_recv()
             pieces = gathered[c].reshape(n * slots, halves, GROUP, LANES)
             lines = [pieces[:, h].reshape(span_rows, LANES) for h in range(halves)]
             high, low = split(jnp.concatenate(lines, axis=1))
@@ -370,8 +419,11 @@
             return carry
 
         lax.fori_loop(0, span_rows // step, body, 0)
-        every_other(me, lambda slab: back_copy(c, slab, who).start())
-        target[cells_of(who, c)] = back[c, block_of(me)]
+        start_back(c)
+
+    def start_back(j):
+        every_other(me, lambda slab: back_copy(j, slab).start())
+        target[extent_of(who, j)] = back[j % chunks, block_of(j, me)]
 
     def sum_y(value):
         pieces = [value[y : y + GROUP, :] for y in range(0, ny, GROUP)]
@@ -403,18 +455,27 @@
             axis=1,
         )
 
-    def collect(c):
-        def body(r, carry):
-            for g in order[c]:
+    def collect(j):
+        def gather(e):
+            def body(r, carry):
                 for h in range(halves):
                     for y in range(0, ny, GROUP):
-                        first = y * deep + ((g + 1) % groups * halves + h) * GROUP + r
-                        goal[PAD + g * GROUP + r, y : y + GROUP, h * LANES : (h + 1) * LANES] = (
-                            target[pl.ds(first, GROUP, stride=deep), :]
-                        )
-            return carry
-
-        lax.fori_loop(0, GROUP, body, 0)
+                        goal[
+                            PAD + (e - 1) * GROUP + r,
+                            y : y + GROUP,
+                            h * LANES : (h + 1) * LANES,
+                        ] = target[pl.ds(y * wide + e * tall + h * GROUP + r, GROUP, stride=wide), :]
+                return carry
+
+            lax.fori_loop(0, GROUP, body, 0)
+
+        for e in range(j * slots, (j + 1) * slots):
+            if e == 0:
+                pl.when(me > 0)(functools.partial(gather, e))
+            elif e == groups + 1:
+                pl.when(me < n - 1)(functools.partial(gather, e))
+            else:
+                gather(e)
 
     def rise_load(origin, x, fresh):
         here, before, after = origin[x], origin[x - 1], origin[x + 1]
@@ -501,30 +562,24 @@
 
     homes = [(x, x + GROUP) for x in range(0, rows, GROUP)]
 
-    def denoise(outer, arrive):
+    def denoise(outer):
         stop = rows + REACH + (1 if outer < OUTER - 1 else 0)
         done = -5 if outer < OUTER - 1 else -3
-        ready = {}
         if outer < OUTER - 1:
-            for c in range(1, chunks):
-                ready[(c * slots + slots - 1) * GROUP + REACH] = c
-            ready[rows + REACH] = 0
+            ready = {batch[2] * GROUP + REACH: batch for batch in batches}
         else:
-            ready = {last + REACH: i for i, (_, last) in enumerate(homes)}
-        for c in range(min(1, chunks - 1), chunks):
-            if c > 0:
-                arrive(c)
-                collect(c)
-            if c == min(1, chunks - 1):
-                halo_done()
-            limit = stop if c == chunks - 1 else (c * slots + slots - 1) * GROUP - 1
+            ready = {last + REACH: (first, last) for first, last in homes}
+        for j in range(extents):
+            back_bulk(j).wait_recv()
+            collect(j)
+            limit = stop if j == extents - 1 else ((j + 1) * slots - 1) * GROUP - 1
             for x in sorted(ready):
                 if done < x <= limit:
                     sweep_rows(outer, done, x)
                     if outer < OUTER - 1:
                         send_forward(ready[x])
                     else:
-                        deliver(ready[x], *homes[ready[x]])
+                        deliver(*ready[x])
                     done = x
             if done < limit:
                 sweep_rows(outer, done, limit)
@@ -533,81 +588,54 @@
     turns = list(range(1, chunks)) + [0]
     lax.fori_loop(0, ny, stage, 0)
     pl.semaphore_wait(barrier, greeted - 1)
-    for c in turns:
-        send_first(c)
+    ahead = min(2, len(first_turn))
+    for batch in first_turn[:ahead]:
+        send_aside(batch)
+    for i, batch in enumerate(first_turn):
+        send_direct(batch)
+        for later in first_turn[i + ahead : i + ahead + 1]:
+            send_aside(later)
 
     @pl.when(me == 0)
     def _():
-        goal[PAD - REACH : PAD] = jnp.zeros((REACH, ny, nz), f32)
+        goal[PAD - GROUP : PAD] = jnp.zeros((GROUP, ny, nz), f32)
 
     @pl.when(me == n - 1)
     def _():
-        goal[PAD + rows : PAD + rows + REACH] = jnp.zeros((REACH, ny, nz), f32)
+        goal[PAD + rows : PAD + rows + GROUP] = jnp.zeros((GROUP, ny, nz), f32)
 
     make_tables()
-    for c in turns[: chunks // 2]:
-        pass_along(c)
+    for batch in first_turn[: len(first_turn) // 2]:
+        pass_along(batch)
     make_filter()
-    for c in turns[chunks // 2 :]:
-        pass_along(c)
-
-    def halo_done():
-        @pl.when(me > 0)
-        def _():
-            halo_copy(0).wait_recv()
-
-        @pl.when(me < n - 1)
-        def _():
-            halo_copy(1).wait_recv()
-
+    for batch in first_turn[len(first_turn) // 2 :]:
+        pass_along(batch)
     for outer in range(OUTER):
         filtered(outer)
         for c in range(chunks):
+            send_back(c)
+        for j in range(chunks, extents):
+            start_back(j)
+        for batch in batches:
             if outer == 0:
-                first_sent(c)
+                first_sent(batch)
             else:
-                every_other(who, lambda owner: forward_copy(c, owner, me, False).wait_send())
-        for c in range(chunks):
-            send_back(c)
-
-        def arrive(c):
-            every_other(who, lambda owner: back_copy(c, me, owner).wait_recv())
-
-        arrive(0)
-        collect(0)
-
-        @pl.when(me < n - 1)
-        def _():
-            halo_copy(0).start()
-
-        @pl.when(me > 0)
-        def _():
-            halo_copy(1).start()
-
-        denoise(outer, arrive)
-
-        @pl.when(me < n - 1)
-        def _():
-            halo_copy(0).wait_send()
-
-        @pl.when(me > 0)
-        def _():
-            halo_copy(1).wait_send()
-
-        for c in range(chunks):
-            every_other(me, lambda slab: back_copy(c, slab, who).wait_send())
-    for i, (first, last) in enumerate(homes):
-        delivered(i, first, last)
-
-
-def constants(n, rows, order, nz):
+                forward_bulk(batch, n - 1).wait_send()
+        denoise(outer)
+        for j in range(extents):
+            back_bulk(j).wait_send()
+    delivered()
+
+
+def constants(n, rows, slots, nz):
     nx = n * rows
+    groups = rows // GROUP
     place = np.array(
         [
-            d * rows + g * GROUP + r
-            for some in order
+            ((d * groups + c + slot - 1) * GROUP + r) % nx
+            for c in range(0, groups, slots)
             for d in range(n)
-            for g in some
+            for slot in range(slots)
             for r in range(GROUP)
         ]
     )
@@ -633,13 +661,12 @@
     rows, ny, nz = observed.shape
     nx = n * rows
     groups = rows // GROUP
-    line = [groups - 1] + list(range(groups - 1))
-    slots = 2 if groups % 2 == 0 else groups
-    order = [tuple(line[c : c + slots]) for c in range(0, groups, slots)]
-    chunks = len(order)
+    slots = 2 if groups % 2 == 0 else 1
+    chunks = groups // slots
+    extents = (groups + 2) // slots
     lines, columns = tilt_index.shape
     depth, width = -(-lines // 128) * 128, -(-columns // 128) * 128
-    tables = constants(n, rows, order, nz)
+    tables = constants(n, rows, slots, nz)
     tiles = observed.reshape(rows, ny // GROUP, GROUP, nz // LANES, LANES)
     tiles = tiles.transpose(0, 1, 3, 2, 4).reshape(-1, LANES)
     vmem = pl.BlockSpec(memory_space=pltpu.VMEM)
@@ -648,9 +675,10 @@
     plane = pltpu.VMEM((nx, nz), f32)
     blocks = pltpu.VMEM((chunks, n * slots * GROUP * nz // LANES, LANES), f32)
     cells = pltpu.VMEM((rows * ny * nz // LANES, LANES), f32)
-    semaphores = pltpu.SemaphoreType.DMA((chunks, n))
+    semaphores = pltpu.SemaphoreType.DMA((extents,))
+    landing = pltpu.VMEM((ny * (groups + 2) * GROUP * nz // LANES, LANES), f32)
     result = pl.pallas_call(
-        functools.partial(kernel, n, rows, order, cross),
+        functools.partial(kernel, n, rows, slots, cross),
         out_shape=jax.ShapeDtypeStruct((rows, ny, nz), f32),
         in_specs=[vmem, smem] + [vmem] * 8,
         out_specs=pl.BlockSpec(memory_space=pl.ANY),
@@ -664,7 +692,7 @@
             pltpu.VMEM((nx, nz), bf16),
             pltpu.VMEM((nx, nz), bf16),
             blocks,
-            cells,
+            landing,
             grid_rows,
             grid_rows,
             grid_rows,
@@ -677,14 +705,12 @@
             semaphores,
             semaphores,
             semaphores,
-            pltpu.SemaphoreType.DMA((2,)),
-            pltpu.SemaphoreType.DMA((2,)),
-            pltpu.SemaphoreType.DMA((chunks, n // 2)),
-            pltpu.SemaphoreType.DMA((chunks, n // 2)),
-            pltpu.SemaphoreType.DMA((chunks, n // 2)),
-            pltpu.SemaphoreType.DMA((groups,)),
-            pltpu.SemaphoreType.DMA((groups,)),
-            pltpu.SemaphoreType.DMA((groups,)),
+            semaphores,
+            semaphores,
+            semaphores,
+            pltpu.SemaphoreType.DMA(()),
+            pltpu.SemaphoreType.DMA(()),
+            pltpu.SemaphoreType.DMA(()),
         ],
         compiler_params=pltpu.CompilerParams(
             collective_id=0, has_side_effects=True, vmem_limit_bytes=60 * 1024 * 1024

time: 132 us -> 110 us (0.83); the launches traced: 130 us -> 110 us
  Pallas kernels: 128 us -> 108 us
    pallas_call x1, Pallas kernels: 128 us -> 108 us  [local(): pl.pallas_call(functools.partial(kernel, n, rows, slots, cross), out_shap...]
where the time goes in v3:
time: 110 us
  Pallas kernels  108 us (98%)
  local copies, waits for them, and re-layouts  2.26 us (2%)
    pallas_call x1, Pallas kernels, local(): pl.pallas_call(functools.partial(kernel, n, rows, slots, cross), out_shap...  108 us
    unnamed x1, local copies, waits for them, and re-layouts  2.26 us

profile of v3, /device:TPU:2, one launch (start us, length us, event | category | flops | bytes accessed | tf_op | source)
XLA Modules:
  0.0 109.9 jit_solution(1948853176028209501)
XLA Ops:
  0.0 107.7 %shard_map.100 = f32[64,16,256]{2,1,0:T(8,128)} custom-call(f32[2048,128]{1,0:T(8,128)} %bitcast.7, f32[16]{0:T(128)} %table_ref.1, s32[129,513]{1,0:T(8,128)} %bitcast.8, s32[129,513]{1,0:T(8,128)} %bitcast.9, f32[128,1024]{1,0:T(8,128)} %constant.12.clone.cos_ref, f32[128,1024]{1,0:T(8,128)} %constant.13.clone.sin_ref, f32[8,1024]{1,0:T(8,128)} %constant.14.clone.cas_ref, ...), custom_call_target="tpu_custom_call" | custom-call | tf_op jit(solution)/shard_map/pallas_call | solution.py:680
  107.7 2.3 %copy.12 = f32[64,16,256]{2,1,0:T(8,128)} copy(f32[64,16,256]{2,1,0:T(8,128)} %shard_map.100) | data formatting | bytes 2097152

commit v4 on v3

--- a/solution.py
+++ b/solution.py
@@ -113,12 +113,17 @@
 
         lax.fori_loop(1, n, step, 0)
 
-    def every_half(action):
+    def every_half(action, start=0, stop=None):
+        count = (half if stop is None else stop) - start
+
         def step(o, carry):
-            action(lax.rem(low + o, half))
+            action(start + lax.rem(low + o, count))
             return carry
 
-        lax.fori_loop(0, half, step, 0)
+        lax.fori_loop(0, count, step, 0)
+
+    def straight(batch):
+        return half // 2 if batch is batches[-1] else 0
 
     def cells_of(y, batch, depth):
         _, low_group, high_group = batch
@@ -245,11 +250,13 @@
 
     def pass_bulk(batch):
         m = batch[0]
-        return bulk(passing, half * lines_of(batch), pass_send.at[m], pass_recv.at[m])
+        count = half - straight(batch)
+        return bulk(passing, count * lines_of(batch), pass_send.at[m], pass_recv.at[m])
 
     def pass_on_bulk(batch):
         m = batch[0]
-        return bulk(passing, half * lines_of(batch), pass_on.at[m], pass_recv.at[m])
+        count = half - straight(batch)
+        return bulk(passing, count * lines_of(batch), pass_on.at[m], pass_recv.at[m])
 
     def back_bulk(j):
         return bulk(target, (n - 1) * share, back_send.at[j], back_recv.at[j])
@@ -263,6 +270,12 @@
             @pl.when(far)
             def _():
                 every_half(lambda k: forward_copy(batch, gx * half + k, gy, True).start())
+                if straight(batch):
+                    every_half(
+                        lambda k: forward_copy(batch, (1 - gx) * half + k, gy, True).start(),
+                        0,
+                        straight(batch),
+                    )
 
         @pl.when(near)
         def _():
@@ -274,7 +287,7 @@
 
             @pl.when(far)
             def _():
-                every_half(lambda k: pass_copy(batch, k).start())
+                every_half(lambda k: pass_copy(batch, k).start(), straight(batch), half)
 
     def pass_along(batch):
         if cross:
@@ -282,7 +295,7 @@
             @pl.when(near)
             def _():
                 pass_bulk(batch).wait_recv()
-                every_half(lambda k: pass_on_copy(batch, k).start())
+                every_half(lambda k: pass_on_copy(batch, k).start(), straight(batch), half)
 
     def first_arrived(batch):
         @pl.when(near)
@@ -306,7 +319,7 @@
 
             @pl.when(far)
             def _():
-                forward_bulk(batch, half).wait_send()
+                forward_bulk(batch, half + straight(batch)).wait_send()
                 pass_bulk(batch).wait_send()
 
     def send_forward(batch):
@@ -401,7 +414,7 @@
                 m_high[at, :], m_low[at, :] = split(dot3(a_high, a_low, zh_ref[...], zl_ref[...]))
                 return carry
 
-            lax.fori_loop(0, row_blocks, body, 0)
+            lax.fori_loop(0, row_blocks, body, 0, unroll=True)
 
     def send_back(c):
         step = math.gcd(span_rows, 256)
@@ -588,12 +601,11 @@
     turns = list(range(1, chunks)) + [0]
     lax.fori_loop(0, ny, stage, 0)
     pl.semaphore_wait(barrier, greeted - 1)
-    ahead = min(2, len(first_turn))
-    for batch in first_turn[:ahead]:
+    for batch in batches[:2]:
         send_aside(batch)
     for i, batch in enumerate(first_turn):
         send_direct(batch)
-        for later in first_turn[i + ahead : i + ahead + 1]:
+        for later in batches[i + 2 : i + 3]:
             send_aside(later)
 
     @pl.when(me == 0)
@@ -605,10 +617,9 @@
         goal[PAD + rows : PAD + rows + GROUP] = jnp.zeros((GROUP, ny, nz), f32)
 
     make_tables()
-    for batch in first_turn[: len(first_turn) // 2]:
-        pass_along(batch)
+    pass_along(batches[0])
     make_filter()
-    for batch in first_turn[len(first_turn) // 2 :]:
+    for batch in batches[1:]:
         pass_along(batch)
     for outer in range(OUTER):
         filtered(outer)

time: 110 us -> 108 us (0.982)
  Pallas kernels: 108 us -> 105 us
    pallas_call x1, Pallas kernels: 108 us -> 105 us  [local(): pl.pallas_call(functools.partial(kernel, n, rows, slots, cross), out_shap...]
where the time goes in v4:
time: 108 us
  Pallas kernels  105 us (97%)
  local copies, waits for them, and re-layouts  2.26 us (2%)
    pallas_call x1, Pallas kernels, local(): pl.pallas_call(functools.partial(kernel, n, rows, slots, cross), out_shap...  105 us
    unnamed x1, local copies, waits for them, and re-layouts  2.26 us

profile of v4, /device:TPU:2, one launch (start us, length us, event | category | flops | bytes accessed | tf_op | source)
XLA Modules:
  0.0 107.7 jit_solution(11673902263888415405)
XLA Ops:
  0.0 105.4 %shard_map.100 = f32[64,16,256]{2,1,0:T(8,128)} custom-call(f32[2048,128]{1,0:T(8,128)} %bitcast.7, f32[16]{0:T(128)} %table_ref.1, s32[129,513]{1,0:T(8,128)} %bitcast.8, s32[129,513]{1,0:T(8,128)} %bitcast.9, f32[128,1024]{1,0:T(8,128)} %constant.12.clone.cos_ref, f32[128,1024]{1,0:T(8,128)} %constant.13.clone.sin_ref, f32[8,1024]{1,0:T(8,128)} %constant.14.clone.cas_ref, ...), custom_call_target="tpu_custom_call" | custom-call | tf_op jit(solution)/shard_map/pallas_call | solution.py:691
  105.4 2.3 %copy.12 = f32[64,16,256]{2,1,0:T(8,128)} copy(f32[64,16,256]{2,1,0:T(8,128)} %shard_map.100) | data formatting | bytes 2097152

commit v5 on v3

--- a/solution.py
+++ b/solution.py
@@ -40,8 +40,9 @@
 
 def kernel(
     n, rows, slots, cross,
-    cells_ref, table_ref, tilt_ref, wedge_ref, cos_ref, sin_ref, cas_ref, case_ref, zh_ref, zl_ref,
+    cells_in, table_ref, tilt_in, wedge_in, cos_in, sin_in, cas_in, case_in, zh_in, zl_in,
     out_ref,
+    cells_ref, tilt_ref, wedge_ref, cos_ref, sin_ref, cas_ref, case_ref, zh_ref, zl_ref, load_sem,
     gathered, total, data_term, prior_gain, x_high, x_low, m_high, m_low, back,
     target, goal, field, lead, duals, current, code, passing, result,
     send_sem, recv_sem, back_send, back_recv,
@@ -85,6 +86,7 @@
         (m, max(m * slots - 1, 0), min((m + 1) * slots - 1, groups))
         for m in range(1 // slots, groups // slots + 1)
     ]
+    aside = batches[:-1]
     first_turn = [batch for batch in batches if batch[0] % chunks > 0]
     first_turn += [batch for batch in batches if batch[0] % chunks == 0]
     nx = n * rows
@@ -104,6 +106,24 @@
         return carry
 
     greeted = 2 * n if cross else n
+    loads = [
+        pltpu.make_async_copy(source, place, load_sem.at[i])
+        for i, (source, place) in enumerate(
+            [
+                (cells_in, cells_ref),
+                (cos_in, cos_ref),
+                (sin_in, sin_ref),
+                (cas_in, cas_ref),
+                (case_in, case_ref),
+                (tilt_in, tilt_ref),
+                (wedge_in, wedge_ref),
+                (zh_in, zh_ref),
+                (zl_in, zl_ref),
+            ]
+        )
+    ]
+    for load in loads:
+        load.start()
     lax.fori_loop(1, greeted, greet, 0)
 
     def every_other(mine, action):
@@ -113,12 +133,14 @@
 
         lax.fori_loop(1, n, step, 0)
 
-    def every_half(action):
+    def every_half(side, action):
+        count = half // 2
+
         def step(o, carry):
-            action(lax.rem(low + o, half))
+            action(lax.rem(low // 2 + o, count) * 2 + side)
             return carry
 
-        lax.fori_loop(0, half, step, 0)
+        lax.fori_loop(0, count, step, 0)
 
     def cells_of(y, batch, depth):
         _, low_group, high_group = batch
@@ -149,13 +171,13 @@
             device_id_type=MESH,
         )
 
-    def pass_copy(batch, k):
+    def pass_copy(batch, side, k):
         m = batch[0]
         return pltpu.make_async_remote_copy(
             src_ref=current.at[cells_of((1 - gx) * half + k, batch, deep)],
             dst_ref=passing.at[cells_of(k, batch, deep)],
-            send_sem=pass_send.at[m],
-            recv_sem=pass_recv.at[m],
+            send_sem=pass_send.at[side, m],
+            recv_sem=pass_recv.at[side, m],
             device_id={"groups": 1 - gx, "gy": gy},
             device_id_type=MESH,
         )
@@ -243,13 +265,13 @@
         m = batch[0]
         return bulk(current, count * lines_of(batch), send_sem.at[m], recv_sem.at[m])
 
-    def pass_bulk(batch):
-        m = batch[0]
-        return bulk(passing, half * lines_of(batch), pass_send.at[m], pass_recv.at[m])
+    def pass_bulk(batch, side):
+        lines = half // 2 * lines_of(batch)
+        return bulk(passing, lines, pass_send.at[side, batch[0]], pass_recv.at[side, batch[0]])
 
     def pass_on_bulk(batch):
         m = batch[0]
-        return bulk(passing, half * lines_of(batch), pass_on.at[m], pass_recv.at[m])
+        return bulk(passing, half * lines_of(batch), pass_on.at[m], pass_recv.at[0, m])
 
     def back_bulk(j):
         return bulk(target, (n - 1) * share, back_send.at[j], back_recv.at[j])
@@ -257,32 +279,48 @@
     def keep_own(batch, slab):
         gathered[batch[0] % chunks, seat_of(slab, batch)] = current[cells_of(who, batch, deep)]
 
-    def send_direct(batch):
+    def send_direct(batch, side):
+        if not cross:
+            if side == 0:
+                every_other(who, lambda owner: forward_copy(batch, owner, gy, True).start())
+                keep_own(batch, gy)
+            return
+
+        @pl.when(far)
+        def _():
+            every_half(side, lambda k: forward_copy(batch, gx * half + k, gy, True).start())
+            if batch not in aside:
+                every_half(
+                    side, lambda k: forward_copy(batch, (1 - gx) * half + k, gy, True).start()
+                )
+
+        @pl.when(near)
+        def _():
+            every_half(side, lambda k: forward_copy(batch, (1 - gx) * half + k, gy, True).start())
+
+            def own_row(k):
+                @pl.when(k != low)
+                def _():
+                    forward_copy(batch, gx * half + k, gy, True).start()
+
+            every_half(side, own_row)
+            if side == 0:
+                keep_own(batch, gy)
+
+    def send_aside(batch, side):
         if cross:
 
             @pl.when(far)
             def _():
-                every_half(lambda k: forward_copy(batch, gx * half + k, gy, True).start())
-
-        @pl.when(near)
-        def _():
-            every_other(who, lambda owner: forward_copy(batch, owner, gy, True).start())
-            keep_own(batch, gy)
-
-    def send_aside(batch):
-        if cross:
-
-            @pl.when(far)
-            def _():
-                every_half(lambda k: pass_copy(batch, k).start())
-
-    def pass_along(batch):
+                every_half(side, lambda k: pass_copy(batch, side, k).start())
+
+    def pass_along(batch, side):
         if cross:
 
             @pl.when(near)
             def _():
-                pass_bulk(batch).wait_recv()
-                every_half(lambda k: pass_on_copy(batch, k).start())
+                pass_bulk(batch, side).wait_recv()
+                every_half(side, lambda k: pass_on_copy(batch, k).start())
 
     def first_arrived(batch):
         @pl.when(near)
@@ -296,18 +334,22 @@
                 forward_bulk(batch, n).wait_recv()
 
     def first_sent(batch):
+        relayed = cross and batch in aside
+
         @pl.when(near)
         def _():
             forward_bulk(batch, n - 1).wait_send()
-            if cross:
+            if relayed:
                 pass_on_bulk(batch).wait_send()
 
         if cross:
 
             @pl.when(far)
             def _():
-                forward_bulk(batch, half).wait_send()
-                pass_bulk(batch).wait_send()
+                forward_bulk(batch, half if relayed else n).wait_send()
+                if relayed:
+                    pass_bulk(batch, 0).wait_send()
+                    pass_bulk(batch, 1).wait_send()
 
     def send_forward(batch):
         every_other(who, lambda owner: forward_copy(batch, owner, me, False).start())
@@ -401,7 +443,7 @@
                 m_high[at, :], m_low[at, :] = split(dot3(a_high, a_low, zh_ref[...], zl_ref[...]))
                 return carry
 
-            lax.fori_loop(0, row_blocks, body, 0)
+            lax.fori_loop(0, row_blocks, body, 0, unroll=True)
 
     def send_back(c):
         step = math.gcd(span_rows, 256)
@@ -586,15 +628,18 @@
                 done = limit
 
     turns = list(range(1, chunks)) + [0]
+    loads[0].wait()
     lax.fori_loop(0, ny, stage, 0)
     pl.semaphore_wait(barrier, greeted - 1)
-    ahead = min(2, len(first_turn))
-    for batch in first_turn[:ahead]:
-        send_aside(batch)
-    for i, batch in enumerate(first_turn):
-        send_direct(batch)
-        for later in first_turn[i + ahead : i + ahead + 1]:
-            send_aside(later)
+    asides = [(batch, side) for side in range(2) for batch in aside]
+    for turn in asides[:2]:
+        send_aside(*turn)
+    for side in range(2):
+        for i, batch in enumerate(first_turn):
+            send_direct(batch, side)
+            at = side * len(aside) + i + 2
+            for turn in asides[at : at + 1] if i < len(aside) else []:
+                send_aside(*turn)
 
     @pl.when(me == 0)
     def _():
@@ -604,12 +649,14 @@
     def _():
         goal[PAD + rows : PAD + rows + GROUP] = jnp.zeros((GROUP, ny, nz), f32)
 
+    for load in loads[1:]:
+        load.wait()
     make_tables()
-    for batch in first_turn[: len(first_turn) // 2]:
-        pass_along(batch)
+    for turn in asides[:1]:
+        pass_along(*turn)
     make_filter()
-    for batch in first_turn[len(first_turn) // 2 :]:
-        pass_along(batch)
+    for turn in asides[1:]:
+        pass_along(*turn)
     for outer in range(OUTER):
         filtered(outer)
         for c in range(chunks):
@@ -671,6 +718,8 @@
     tiles = tiles.transpose(0, 1, 3, 2, 4).reshape(-1, LANES)
     vmem = pl.BlockSpec(memory_space=pltpu.VMEM)
     smem = pl.BlockSpec(memory_space=pltpu.SMEM)
+    hbm = pl.BlockSpec(memory_space=pltpu.HBM)
+    operands = (tiles, tilt_index.T, wedge.T, *tables)
     grid_rows = pltpu.VMEM((rows + 2 * PAD, ny, nz), f32)
     plane = pltpu.VMEM((nx, nz), f32)
     blocks = pltpu.VMEM((chunks, n * slots * GROUP * nz // LANES, LANES), f32)
@@ -679,10 +728,12 @@
     landing = pltpu.VMEM((ny * (groups + 2) * GROUP * nz // LANES, LANES), f32)
     result = pl.pallas_call(
         functools.partial(kernel, n, rows, slots, cross),
-        out_shape=jax.ShapeDtypeStruct((rows, ny, nz), f32),
-        in_specs=[vmem, smem] + [vmem] * 8,
-        out_specs=pl.BlockSpec(memory_space=pl.ANY),
-        scratch_shapes=[
+        out_shape=pltpu.VMEM((rows, ny, nz), f32),
+        in_specs=[hbm, smem] + [hbm] * 8,
+        out_specs=vmem,
+        scratch_shapes=[pltpu.VMEM(operand.shape, operand.dtype) for operand in operands]
+        + [
+            pltpu.SemaphoreType.DMA((len(operands),)),
             blocks,
             plane,
             plane,
@@ -705,8 +756,8 @@
             semaphores,
             semaphores,
             semaphores,
-            semaphores,
-            semaphores,
+            pltpu.SemaphoreType.DMA((2, extents)),
+            pltpu.SemaphoreType.DMA((2, extents)),
             semaphores,
             pltpu.SemaphoreType.DMA(()),
             pltpu.SemaphoreType.DMA(()),
@@ -715,7 +766,7 @@
         compiler_params=pltpu.CompilerParams(
             collective_id=0, has_side_effects=True, vmem_limit_bytes=60 * 1024 * 1024
         ),
-    )(tiles, tf_table, tilt_index.T, wedge.T, *tables)
+    )(operands[0], tf_table, *operands[1:])
     return result
 
 

time: 110 us -> 101 us (0.918)
  Pallas kernels: 108 us -> 99.9 us
  local copies, waits for them, and re-layouts: 2.26 us -> 0.97 us
    pallas_call x1, Pallas kernels: 108 us -> 99.9 us  [local(): pl.pallas_call(functools.partial(kernel, n, rows, slots, cross), out_shap...]
    unnamed x1, local copies, waits for them, and re-layouts: 2.26 us -> 0.97 us
where the time goes in v5:
time: 101 us
  Pallas kernels  99.9 us (99%)
    pallas_call x1, Pallas kernels, local(): pl.pallas_call(functools.partial(kernel, n, rows, slots, cross), out_shap...  99.9 us

profile of v5, /device:TPU:2, one launch (start us, length us, event | category | flops | bytes accessed | tf_op | source)
XLA Modules:
  0.0 100.9 jit_solution(12122179503075760760)
XLA Ops:
  0.0 99.9 %shard_map.100 = f32[64,16,256]{2,1,0:T(8,128)S(1)} custom-call(f32[2048,128]{1,0:T(8,128)} %bitcast.7, f32[16]{0:T(128)} %table_ref.1, s32[129,513]{1,0:T(8,128)} %bitcast.8, s32[129,513]{1,0:T(8,128)} %bitcast.9, f32[128,1024]{1,0:T(8,128)} %constant.12.clone.cos_in, f32[128,1024]{1,0:T(8,128)} %constant.13.clone.sin_in, f32[8,1024]{1,0:T(8,128)} %constant.14.clone.cas_in, ...), custom_call_target="tpu_custom_call" | custom-call | tf_op jit(solution)/shard_map/pallas_call | solution.py:729
  100.0 1.0 copy.12

commit v6 on v5

--- a/solution.py
+++ b/solution.py
@@ -9,11 +9,14 @@
 from jax.experimental.pallas import tpu as pltpu
 from jax.sharding import PartitionSpec as P
 
+WAVES = 2
 OUTER = 2
 PASSES = 2
 GROUP = 8
 LANES = 128
-REACH = 6
+WIDE = 2
+LAG = WIDE + 1
+DELAY = 3 * LAG
 PAD = 12
 
 step_dual = 0.14
@@ -134,10 +137,10 @@
         lax.fori_loop(1, n, step, 0)
 
     def every_half(side, action):
-        count = half // 2
+        count = half // WAVES
 
         def step(o, carry):
-            action(lax.rem(low // 2 + o, count) * 2 + side)
+            action(lax.rem(low // WAVES + o, count) * WAVES + side)
             return carry
 
         lax.fori_loop(0, count, step, 0)
@@ -266,7 +269,7 @@
         return bulk(current, count * lines_of(batch), send_sem.at[m], recv_sem.at[m])
 
     def pass_bulk(batch, side):
-        lines = half // 2 * lines_of(batch)
+        lines = half // WAVES * lines_of(batch)
         return bulk(passing, lines, pass_send.at[side, batch[0]], pass_recv.at[side, batch[0]])
 
     def pass_on_bulk(batch):
@@ -348,12 +351,22 @@
             def _():
                 forward_bulk(batch, half if relayed else n).wait_send()
                 if relayed:
-                    pass_bulk(batch, 0).wait_send()
-                    pass_bulk(batch, 1).wait_send()
-
-    def send_forward(batch):
-        every_other(who, lambda owner: forward_copy(batch, owner, me, False).start())
-        keep_own(batch, me)
+                    for side in range(WAVES):
+                        pass_bulk(batch, side).wait_send()
+
+    def send_forward(batch, side):
+        def step(o, carry):
+            owner = lax.rem(who // 2 + o, half) * 2 + side
+
+            @pl.when(owner != who)
+            def _():
+                forward_copy(batch, owner, me, False).start()
+
+            return carry
+
+        lax.fori_loop(0, half, step, 0)
+        if side == 0:
+            keep_own(batch, me)
 
     def stage(y, carry):
         stride = ny * halves
@@ -552,65 +565,83 @@
 
     def sweep_rows(outer, start, stop):
         def run(first, last):
-            masked = first < REACH or last > rows
-            ends = first >= REACH and last <= rows + REACH
+            masked = first < DELAY or last > rows - WIDE + 1
+            ends = first >= DELAY and last <= rows + DELAY
+            lines = range(WIDE)
 
             def keep(x):
-                if not masked:
-                    return None
                 whole = me * rows + PAD + x
                 return jnp.where(jnp.logical_and(whole >= 2 * PAD, whole < nx + 2 * PAD), 1.0, 0.0)
 
-            def body(x, carry):
-                low = rise_load(goal, x, outer == 0)
-                mid = fall_load(x - 2)
-                high = rise_load(lead, x - 4, False)
+            def body(k, carry):
+                x = k * WIDE + (first + PAD)
+                low = [rise_load(goal, x + i, outer == 0) for i in lines]
+                mid = [fall_load(x - LAG + i) for i in lines]
+                high = [rise_load(lead, x - 2 * LAG + i, False) for i in lines]
                 if ends:
-                    top = fall_load(x - 6)
-                    old = field[x - 6]
-                fresh = rise(low, keep(x))
-                updated = mid[-1] - fall(mid)
+                    top = [fall_load(x - DELAY + i) for i in lines]
+                    old = [field[x - DELAY + i] for i in lines]
+                fresh = [rise(low[i], keep(x + i) if masked else None) for i in lines]
+                updated = [mid[i][-1] - fall(mid[i]) for i in lines]
                 if masked:
-                    updated = updated * keep(x - 2)
-                again = rise(high, keep(x - 4))
+                    updated = [updated[i] * keep(x - LAG + i) for i in lines]
+                again = [
+                    rise(high[i], keep(x - 2 * LAG + i) if masked else None) for i in lines
+                ]
                 if ends:
-                    final = (
-                        old * (1.0 / (1.0 + step_primal))
-                        + top[-1] * (step_primal / (1.0 + step_primal))
-                        - fall(top)
-                    )
-                for dual, value in zip(duals, fresh):
-                    dual[x] = value
-                lead[x - 2] = updated + updated - mid[-1]
-                field[x - 2] = updated
-                for dual, value in zip(duals, again):
-                    dual[x - 4] = value
-                if ends and outer == OUTER - 1:
-                    result[x - PAD - 6] = final * (1.0 / gain)
-                elif ends:
-                    for h in range(halves):
-                        at = cell_row(x - PAD - 6, h)
-                        for y in range(0, ny, GROUP):
-                            current[pl.ds(at + y * deep, GROUP, stride=deep), :] = final[
-                                y : y + GROUP, h * LANES : (h + 1) * LANES
-                            ]
+                    final = [
+                        old[i] * (1.0 / (1.0 + step_primal))
+                        + top[i][-1] * (step_primal / (1.0 + step_primal))
+                        - fall(top[i])
+                        for i in lines
+                    ]
+                for i in lines:
+                    for dual, value in zip(duals, fresh[i]):
+                        dual[x + i] = value
+                    lead[x - LAG + i] = updated[i] + updated[i] - mid[i][-1]
+                    field[x - LAG + i] = updated[i]
+                    for dual, value in zip(duals, again[i]):
+                        dual[x - 2 * LAG + i] = value
+                for i in lines:
+                    at_x = x + i - PAD - DELAY
+                    if ends and outer == OUTER - 1:
+                        result[at_x] = final[i] * (1.0 / gain)
+                    elif ends:
+                        for h in range(halves):
+                            at = cell_row(at_x, h)
+                            for y in range(0, ny, GROUP):
+                                current[pl.ds(at + y * deep, GROUP, stride=deep), :] = final[i][
+                                    y : y + GROUP, h * LANES : (h + 1) * LANES
+                                ]
                 return carry
 
-            lax.fori_loop(first + PAD, last + PAD, body, 0)
-
-        marks = [start] + [x for x in (REACH, rows, rows + REACH) if start < x < stop] + [stop]
+            lax.fori_loop(0, (last - first) // WIDE, body, 0)
+
+        cuts = {x for x in (DELAY, rows - WIDE + 1, rows + DELAY) if start < x < stop}
+        marks = sorted(cuts | {start, stop})
         for first, last in zip(marks[:-1], marks[1:]):
             run(first, last)
 
     homes = [(x, x + GROUP) for x in range(0, rows, GROUP)]
 
-    def denoise(outer):
-        stop = rows + REACH + (1 if outer < OUTER - 1 else 0)
+    def denoise(outer, sent):
+        stop = rows + DELAY + (1 if WIDE == 1 and outer < OUTER - 1 else 0)
+        held = []
         done = -5 if outer < OUTER - 1 else -3
         if outer < OUTER - 1:
-            ready = {batch[2] * GROUP + REACH: batch for batch in batches}
+            ready = {batch[2] * GROUP + DELAY: batch for batch in batches}
         else:
-            ready = {last + REACH: (first, last) for first, last in homes}
+            ready = {last + DELAY: (first, last) for first, last in homes}
+        def later(j):
+            if j < chunks:
+                send_back(j)
+            elif j < extents:
+                start_back(j)
+
+        if sent == chunks:
+            for j in range(sent, extents):
+                later(j)
+            sent = extents
         for j in range(extents):
             back_bulk(j).wait_recv()
             collect(j)
@@ -619,22 +650,28 @@
                 if done < x <= limit:
                     sweep_rows(outer, done, x)
                     if outer < OUTER - 1:
-                        send_forward(ready[x])
+                        send_forward(ready[x], 0)
+                        for batch in held:
+                            send_forward(batch, 1)
+                        held = [ready[x]]
                     else:
                         deliver(*ready[x])
                     done = x
             if done < limit:
                 sweep_rows(outer, done, limit)
                 done = limit
+            later(j + sent)
+        for batch in held:
+            send_forward(batch, 1)
 
     turns = list(range(1, chunks)) + [0]
     loads[0].wait()
     lax.fori_loop(0, ny, stage, 0)
     pl.semaphore_wait(barrier, greeted - 1)
-    asides = [(batch, side) for side in range(2) for batch in aside]
+    asides = [(batch, side) for side in range(WAVES) for batch in aside]
     for turn in asides[:2]:
         send_aside(*turn)
-    for side in range(2):
+    for side in range(WAVES):
         for i, batch in enumerate(first_turn):
             send_direct(batch, side)
             at = side * len(aside) + i + 2
@@ -659,16 +696,15 @@
         pass_along(*turn)
     for outer in range(OUTER):
         filtered(outer)
-        for c in range(chunks):
-            send_back(c)
-        for j in range(chunks, extents):
-            start_back(j)
+        lead_in = chunks if outer < OUTER - 1 else min(chunks, 3)
+        for j in range(lead_in):
+            send_back(j)
         for batch in batches:
             if outer == 0:
                 first_sent(batch)
             else:
                 forward_bulk(batch, n - 1).wait_send()
-        denoise(outer)
+        denoise(outer, lead_in)
         for j in range(extents):
             back_bulk(j).wait_send()
     delivered()
@@ -756,8 +792,8 @@
             semaphores,
             semaphores,
             semaphores,
-            pltpu.SemaphoreType.DMA((2, extents)),
-            pltpu.SemaphoreType.DMA((2, extents)),
+            pltpu.SemaphoreType.DMA((WAVES, extents)),
+            pltpu.SemaphoreType.DMA((WAVES, extents)),
             semaphores,
             pltpu.SemaphoreType.DMA(()),
             pltpu.SemaphoreType.DMA(()),
@@ -774,6 +810,6 @@
     in_specs = (P(("groups", "gy"), None, None), P(), P(), P())
     out_specs = P(("groups", "gy"), None, None)
     n = mesh.shape["gy"]
-    cross = mesh.shape["groups"] == 2 and n % 4 == 0
+    cross = mesh.shape["groups"] == 2 and n % (2 * WAVES) == 0
     body = functools.partial(local, n, cross)
     return jax.shard_map(body, mesh=mesh, in_specs=in_specs, out_specs=out_specs, check_vma=False)

time: 101 us -> 98.6 us (0.976)
  Pallas kernels: 99.9 us -> 96.9 us
    pallas_call x1, Pallas kernels: 99.9 us -> 96.9 us  [local(): pl.pallas_call(functools.partial(kernel, n, rows, slots, cross), out_shap...]
where the time goes in v6:
time: 98.6 us; the launch traced here: 97.9 us
  Pallas kernels  96.9 us (98%)
    pallas_call x1, Pallas kernels, local(): pl.pallas_call(functools.partial(kernel, n, rows, slots, cross), out_shap...  96.9 us

profile of v6, /device:TPU:2, one launch (start us, length us, event | category | flops | bytes accessed | tf_op | source)
XLA Modules:
  0.0 97.9 jit_solution(12148496899860402238)
XLA Ops:
  0.0 96.9 %shard_map.100 = f32[64,16,256]{2,1,0:T(8,128)S(1)} custom-call(f32[2048,128]{1,0:T(8,128)} %bitcast.7, f32[16]{0:T(128)} %table_ref.1, s32[129,513]{1,0:T(8,128)} %bitcast.8, s32[129,513]{1,0:T(8,128)} %bitcast.9, f32[128,1024]{1,0:T(8,128)} %constant.12.clone.cos_in, f32[128,1024]{1,0:T(8,128)} %constant.13.clone.sin_in, f32[8,1024]{1,0:T(8,128)} %constant.14.clone.cas_in, ...), custom_call_target="tpu_custom_call" | custom-call | tf_op jit(solution)/shard_map/pallas_call | solution.py:765
  96.9 1.0 copy.12

commit v7 on v6

--- a/solution.py
+++ b/solution.py
@@ -651,9 +651,7 @@
                     sweep_rows(outer, done, x)
                     if outer < OUTER - 1:
                         send_forward(ready[x], 0)
-                        for batch in held:
-                            send_forward(batch, 1)
-                        held = [ready[x]]
+                        held.append(ready[x])
                     else:
                         deliver(*ready[x])
                     done = x

time: 98.6 us -> 97.5 us (0.989)
  no operation moved by 1% of the time
where the time goes in v7:
time: 97.5 us; the launch traced here: 97.1 us
  Pallas kernels  96.1 us (99%)
    pallas_call x1, Pallas kernels, local(): pl.pallas_call(functools.partial(kernel, n, rows, slots, cross), out_shap...  96.1 us

profile of v7, /device:TPU:2, one launch (start us, length us, event | category | flops | bytes accessed | tf_op | source)
XLA Modules:
  0.0 97.1 jit_solution(5669572300513168926)
XLA Ops:
  0.0 96.1 %shard_map.100 = f32[64,16,256]{2,1,0:T(8,128)S(1)} custom-call(f32[2048,128]{1,0:T(8,128)} %bitcast.7, f32[16]{0:T(128)} %table_ref.1, s32[129,513]{1,0:T(8,128)} %bitcast.8, s32[129,513]{1,0:T(8,128)} %bitcast.9, f32[128,1024]{1,0:T(8,128)} %constant.12.clone.cos_in, f32[128,1024]{1,0:T(8,128)} %constant.13.clone.sin_in, f32[8,1024]{1,0:T(8,128)} %constant.14.clone.cas_in, ...), custom_call_target="tpu_custom_call" | custom-call | tf_op jit(solution)/shard_map/pallas_call | solution.py:763
  96.1 1.0 %copy.12 = f32[64,16,256]{2,1,0:T(8,128)} copy(f32[64,16,256]{2,1,0:T(8,128)S(1)} %shard_map.100) | data formatting | bytes 2097152

commit v8 on v7

--- a/solution.py
+++ b/solution.py
@@ -134,7 +134,7 @@
             action(lax.rem(mine + o, n))
             return carry
 
-        lax.fori_loop(1, n, step, 0)
+        lax.fori_loop(1, n, step, 0, unroll=5 if n % 5 == 1 else 1)
 
     def every_half(side, action):
         count = half // WAVES

time: 97.5 us -> 97.7 us (level)
  no operation moved by 1% of the time
where the time goes in v8:
time: 97.7 us; the launch traced here: 97.5 us
  Pallas kernels  96.6 us (99%)
    pallas_call x1, Pallas kernels, local(): pl.pallas_call(functools.partial(kernel, n, rows, slots, cross), out_shap...  96.6 us

profile of v8, /device:TPU:2, one launch (start us, length us, event | category | flops | bytes accessed | tf_op | source)
XLA Modules:
  0.0 97.5 jit_solution(11751573836053213273)
XLA Ops:
  0.0 96.6 %shard_map.100 = f32[64,16,256]{2,1,0:T(8,128)S(1)} custom-call(f32[2048,128]{1,0:T(8,128)} %bitcast.7, f32[16]{0:T(128)} %table_ref.1, s32[129,513]{1,0:T(8,128)} %bitcast.8, s32[129,513]{1,0:T(8,128)} %bitcast.9, f32[128,1024]{1,0:T(8,128)} %constant.12.clone.cos_in, f32[128,1024]{1,0:T(8,128)} %constant.13.clone.sin_in, f32[8,1024]{1,0:T(8,128)} %constant.14.clone.cas_in, ...), custom_call_target="tpu_custom_call" | custom-call | tf_op jit(solution)/shard_map/pallas_call | solution.py:763
  96.6 1.0 copy.12
